TPU v7x, 32 devices: a whole 2x2x4 slice. The times are simulated.
32 devices in a mesh: dp: 8 (over y, x, core), ctx: 4 (over z).
Axes of the slice: x: 2, y: 2, z: 4, core: 2. Of those that a mesh axis runs over, the one named last changes fastest.
Arguments:
- hidden_in: float32 [8, 512, 960], P('dp', 'ctx'), may hold values from -6 to 6
- segments: int32 [8, 512], P('dp'), may hold values from 0 to 3, never falling along the last dimension, each value on 1 to 256 neighbouring positions
- attn_flat: bfloat16 [19200, 128], P(('dp', 'ctx')), may hold values from -6 to 6
- mlp_flat: bfloat16 [57600, 128], P(('dp', 'ctx')), may hold values from -6 to 6
- norm_one: float32 [960], replicated, may hold values from 0.1 to 1.9
- norm_two: float32 [960], replicated, may hold values from 0.1 to 1.9
- cotangent: float32 [8, 512, 960], P('dp', 'ctx'), may hold values from -6 to 6
Outputs:
- block_out: float32 [8, 512, 960], P('dp', 'ctx')
- grad_in: float32 [8, 512, 960], P('dp', 'ctx')
- attn_grad: float32 [19200, 128], P(('dp', 'ctx'))
- mlp_grad: float32 [57600, 128], P(('dp', 'ctx'))
- norm_one_grad: float32 [960], replicated
- norm_two_grad: float32 [960], replicated
Inputs may be any that keep to these rules, and one draw needn't show every extreme that they name: `segments`: segment numbers never fall along a sequence; each document covers at most 256 positions, some document exactly that many.
All inputs are finite; a program needn't handle non-finite values.
Results may differ from a plain program's by a relative error of at most 0.015.
Values may be sent and summed in bfloat16 or wider, within the bound.
No kernel may reach another device: no remote copies, remote signals or barrier semaphores. Data moves between devices by JAX's collectives and lax.ppermute only.
A program may use at most 128 MiB of HBM per device.

v0:
```python
import jax
import jax.numpy as jnp
from jax import lax
from jax.sharding import PartitionSpec as P

D = 960
HEADS = 15
KV_HEADS = 5
HEAD_DIM = 64
FFN = 2560


EPS = 1e-05
THETA = 100000.0


def positions_of(segment_ids):
    earlier = (segment_ids[..., None, :] < segment_ids[..., :, None]).astype(jnp.int32)
    total_len = segment_ids.shape[-1]
    return jnp.arange(total_len, dtype=jnp.int32) - jnp.sum(earlier, axis=-1)


def rope_tables(positions):
    half_dim = HEAD_DIM // 2
    frequency = THETA ** (-2.0 * jnp.arange(half_dim, dtype=jnp.float32) / HEAD_DIM)
    angles = positions.astype(jnp.float32)[:, None] * frequency[None, :]
    return (jnp.cos(angles)[:, None, :], jnp.sin(angles)[:, None, :])


def rotate(vectors, cosine_table, sine_table):
    half_dim = vectors.shape[-1] // 2
    lower_half = vectors[..., :half_dim]
    upper_half = vectors[..., half_dim:]
    return jnp.concatenate(
        [
            lower_half * cosine_table - upper_half * sine_table,
            upper_half * cosine_table + lower_half * sine_table,
        ],
        axis=-1,
    )


def unrotate(grad_rows, cosine_table, sine_table):
    half_dim = grad_rows.shape[-1] // 2
    lower_half = grad_rows[..., :half_dim]
    upper_half = grad_rows[..., half_dim:]
    return jnp.concatenate(
        [
            lower_half * cosine_table + upper_half * sine_table,
            upper_half * cosine_table - lower_half * sine_table,
        ],
        axis=-1,
    )


def unpack_blocks(flat_rows, shapes, dp_count, ctx_count):
    pieces = flat_rows.reshape(dp_count, ctx_count, -1).transpose(1, 0, 2).reshape(ctx_count, -1)
    matrices = []
    offset = 0
    for height, width_cols in shapes:
        length = height * width_cols // ctx_count
        matrices.append(pieces[:, offset : offset + length].reshape(height, width_cols))
        offset = offset + length
    return matrices


def norm_forward(residual, gain_vec):
    inverse = lax.rsqrt(jnp.mean(residual * residual, axis=-1, keepdims=True) + EPS)
    return (inverse, residual * inverse * gain_vec)


def norm_backward(residual, inverse, gain_vec, grad_normed):
    scaled = grad_normed * gain_vec
    cubed = inverse * inverse * inverse
    grad_resid = inverse * scaled - residual * cubed * jnp.mean(
        scaled * residual, axis=-1, keepdims=True
    )
    grad_gain = jnp.sum(grad_normed * residual * inverse, axis=0)
    return (grad_resid, grad_gain)


def masked_scores(query_rot, key_whole, allowed, score_scale):
    scores = (
        jnp.einsum("sqkgd,slkd->skgql", query_rot, key_whole, preferred_element_type=jnp.float32)
        * score_scale
    )
    return jnp.where(allowed, scores, -jnp.inf)


def left_dot(left_cols, right_rows):
    return lax.dot_general(
        left_cols, right_rows, (((0,), (0,)), ((), ())), preferred_element_type=jnp.float32
    )


def body(hidden_in, segments, attn_flat, mlp_flat, norm_one, norm_two, cotangent):
    seq_count, local_len, model_width = hidden_in.shape
    seq_len = segments.shape[1]
    row_count = seq_count * local_len
    groups = HEADS // KV_HEADS
    qwidth = HEADS * HEAD_DIM
    kwidth = KV_HEADS * HEAD_DIM
    score_scale = HEAD_DIM ** (-0.5)
    low = jnp.bfloat16
    wide = jnp.float32
    dp_count = lax.axis_size("dp")
    ctx_count = lax.axis_size("ctx")
    attn_shapes = ((D, qwidth), (D, kwidth), (D, kwidth), (qwidth, D))
    mlp_shapes = ((D, FFN), (D, FFN), (FFN, D))
    start_row = lax.axis_index("ctx") * local_len
    attn_whole, mlp_whole = (
        lax.all_gather(attn_flat, ("dp", "ctx"), axis=0, tiled=True),
        lax.all_gather(mlp_flat, ("dp", "ctx"), axis=0, tiled=True),
    )
    w_query, w_key, w_value, w_out = unpack_blocks(attn_whole, attn_shapes, dp_count, ctx_count)
    w_gate, w_up, w_down = unpack_blocks(mlp_whole, mlp_shapes, dp_count, ctx_count)
    pos_all = positions_of(segments)
    pos_local = lax.dynamic_slice_in_dim(pos_all, start_row, local_len, 1)
    seg_local = lax.dynamic_slice_in_dim(segments, start_row, local_len, 1)
    cosine_table, sine_table = rope_tables(pos_local.reshape(-1))
    key_index = jnp.arange(seq_len, dtype=jnp.int32)
    query_index = start_row + jnp.arange(local_len, dtype=jnp.int32)
    allowed = (seg_local[:, :, None] == segments[:, None, :]) & (
        key_index[None, None, :] <= query_index[None, :, None]
    )
    allowed = allowed[:, None, None]
    residual = hidden_in.reshape(row_count, model_width)
    inv_one, normed_one = norm_forward(residual, norm_one)
    normed_one = normed_one.astype(low)
    query = jnp.dot(normed_one, w_query, preferred_element_type=wide).reshape(
        row_count, HEADS, HEAD_DIM
    )
    key_raw = jnp.dot(normed_one, w_key, preferred_element_type=wide).reshape(
        row_count, KV_HEADS, HEAD_DIM
    )
    value_low = jnp.dot(normed_one, w_value, preferred_element_type=wide).astype(low)
    query_rot = (
        rotate(query, cosine_table, sine_table)
        .astype(low)
        .reshape(seq_count, local_len, KV_HEADS, groups, HEAD_DIM)
    )
    key_rot = rotate(key_raw, cosine_table, sine_table).astype(low)
    kv_local = jnp.concatenate(
        [
            key_rot.reshape(seq_count, local_len, kwidth),
            value_low.reshape(seq_count, local_len, kwidth),
        ],
        axis=2,
    )
    kv_whole = lax.all_gather(kv_local, "ctx", axis=1, tiled=True)
    key_whole = kv_whole[:, :, :kwidth].reshape(seq_count, seq_len, KV_HEADS, HEAD_DIM)
    value_whole = kv_whole[:, :, kwidth:].reshape(seq_count, seq_len, KV_HEADS, HEAD_DIM)
    scores = masked_scores(query_rot, key_whole, allowed, score_scale)
    row_top = jnp.max(scores, axis=-1, keepdims=True)
    log_total = row_top + jnp.log(jnp.sum(jnp.exp(scores - row_top), axis=-1, keepdims=True))
    probs_low = jnp.exp(scores - log_total).astype(low)
    head_mix = jnp.einsum("skgql,slkd->sqkgd", probs_low, value_whole, preferred_element_type=wide)
    head_mix = head_mix.reshape(row_count, qwidth).astype(low)
    middle = residual + jnp.dot(head_mix, w_out, preferred_element_type=wide)
    inv_two, normed_two = norm_forward(middle, norm_two)
    normed_two = normed_two.astype(low)
    gate_pre = jnp.dot(normed_two, w_gate, preferred_element_type=wide)
    up_proj = jnp.dot(normed_two, w_up, preferred_element_type=wide)
    gate_sigmoid = jax.nn.sigmoid(gate_pre)
    active = (gate_pre * gate_sigmoid * up_proj).astype(low)
    block_rows = middle + jnp.dot(active, w_down, preferred_element_type=wide)
    one_cols, mix_cols, two_cols, active_cols = (
        lax.all_to_all(normed_one, "ctx", split_axis=1, concat_axis=0, tiled=True),
        lax.all_to_all(head_mix, "ctx", split_axis=1, concat_axis=0, tiled=True),
        lax.all_to_all(normed_two, "ctx", split_axis=1, concat_axis=0, tiled=True),
        lax.all_to_all(active, "ctx", split_axis=1, concat_axis=0, tiled=True),
    )
    cot_rows = cotangent.reshape(row_count, model_width)
    cot_low = cot_rows.astype(low)
    grad_active = jnp.dot(cot_low, w_down.T, preferred_element_type=wide)
    grad_gate = (
        grad_active * up_proj * gate_sigmoid * (1.0 + gate_pre * (1.0 - gate_sigmoid))
    ).astype(low)
    grad_up = (grad_active * gate_pre * gate_sigmoid).astype(low)
    grad_normed_two = jnp.dot(grad_gate, w_gate.T, preferred_element_type=wide) + jnp.dot(
        grad_up, w_up.T, preferred_element_type=wide
    )
    grad_middle, grad_gain_two = norm_backward(middle, inv_two, norm_two, grad_normed_two)
    grad_middle = cot_rows + grad_middle
    grad_mid_low = grad_middle.astype(low)
    grad_mix = jnp.dot(grad_mid_low, w_out.T, preferred_element_type=wide).astype(low)
    grad_mix = grad_mix.reshape(seq_count, local_len, KV_HEADS, groups, HEAD_DIM)
    attn_probs = jnp.exp(masked_scores(query_rot, key_whole, allowed, score_scale) - log_total)
    probs_low = attn_probs.astype(low)
    grad_probs = jnp.einsum("sqkgd,slkd->skgql", grad_mix, value_whole, preferred_element_type=wide)
    grad_value_all = jnp.einsum(
        "skgql,sqkgd->slkd", probs_low, grad_mix, preferred_element_type=wide
    )
    grad_scores = attn_probs * (
        grad_probs - jnp.sum(attn_probs * grad_probs, axis=-1, keepdims=True)
    )
    grad_scores_low = (grad_scores * score_scale).astype(low)
    grad_query = jnp.einsum(
        "skgql,slkd->sqkgd", grad_scores_low, key_whole, preferred_element_type=wide
    )
    grad_key_all = jnp.einsum(
        "skgql,sqkgd->slkd", grad_scores_low, query_rot, preferred_element_type=wide
    )
    kv_terms = jnp.concatenate(
        [
            grad_key_all.reshape(seq_count, seq_len, kwidth),
            grad_value_all.reshape(seq_count, seq_len, kwidth),
        ],
        axis=2,
    )
    kv_owned = lax.psum_scatter(
        kv_terms.astype(jnp.bfloat16), "ctx", scatter_dimension=1, tiled=True
    ).astype(jnp.float32)
    grad_key = kv_owned[:, :, :kwidth].reshape(row_count, KV_HEADS, HEAD_DIM)
    grad_value = kv_owned[:, :, kwidth:].reshape(row_count, kwidth).astype(low)
    grad_query = (
        unrotate(grad_query.reshape(row_count, HEADS, HEAD_DIM), cosine_table, sine_table)
        .reshape(row_count, qwidth)
        .astype(low)
    )
    grad_key = unrotate(grad_key, cosine_table, sine_table).reshape(row_count, kwidth).astype(low)
    grad_normed_one = (
        jnp.dot(grad_query, w_query.T, preferred_element_type=wide)
        + jnp.dot(grad_key, w_key.T, preferred_element_type=wide)
        + jnp.dot(grad_value, w_value.T, preferred_element_type=wide)
    )
    grad_resid, grad_gain_one = norm_backward(residual, inv_one, norm_one, grad_normed_one)
    grad_resid = grad_middle + grad_resid
    gathered = (
        lax.all_gather(grad_query, "ctx", axis=0, tiled=True),
        lax.all_gather(grad_key, "ctx", axis=0, tiled=True),
        lax.all_gather(grad_value, "ctx", axis=0, tiled=True),
        lax.all_gather(grad_mid_low, "ctx", axis=0, tiled=True),
        lax.all_gather(grad_gate, "ctx", axis=0, tiled=True),
        lax.all_gather(grad_up, "ctx", axis=0, tiled=True),
        lax.all_gather(cot_low, "ctx", axis=0, tiled=True),
    )
    all_query, all_key, all_value, all_mid, all_gate, all_up, all_cot = gathered
    attn_terms = jnp.concatenate(
        [
            left_dot(one_cols, all_query).reshape(-1),
            left_dot(one_cols, all_key).reshape(-1),
            left_dot(one_cols, all_value).reshape(-1),
            left_dot(mix_cols, all_mid).reshape(-1),
        ]
    ).reshape(-1, 128)
    mlp_terms = jnp.concatenate(
        [
            left_dot(two_cols, all_gate).reshape(-1),
            left_dot(two_cols, all_up).reshape(-1),
            left_dot(active_cols, all_cot).reshape(-1),
        ]
    ).reshape(-1, 128)
    attn_grad, mlp_grad = (
        lax.psum_scatter(
            attn_terms.astype(jnp.bfloat16), "dp", scatter_dimension=0, tiled=True
        ).astype(jnp.float32),
        lax.psum_scatter(
            mlp_terms.astype(jnp.bfloat16), "dp", scatter_dimension=0, tiled=True
        ).astype(jnp.float32),
    )
    gain_sums = lax.psum(jnp.stack([grad_gain_one, grad_gain_two]), ("dp", "ctx"))
    return (
        block_rows.reshape(seq_count, local_len, model_width),
        grad_resid.reshape(seq_count, local_len, model_width),
        attn_grad,
        mlp_grad,
        gain_sums[0],
        gain_sums[1],
    )


def solution(mesh):
    in_specs = (
        P("dp", "ctx", None),
        P("dp", None),
        P(("dp", "ctx"), None),
        P(("dp", "ctx"), None),
        P(),
        P(),
        P("dp", "ctx", None),
    )
    out_specs = (
        P("dp", "ctx", None),
        P("dp", "ctx", None),
        P(("dp", "ctx"), None),
        P(("dp", "ctx"), None),
        P(),
        P(),
    )
    return jax.shard_map(body, mesh=mesh, in_specs=in_specs, out_specs=out_specs, check_vma=False)
```

profile of v0, /device:TPU:0, one launch (start us, length us, event | category | flops | bytes accessed | tf_op | source)
XLA Modules:
  0.0 637.1 jit_solution(12020990512070765392)
XLA Ops:
  14.3 63.6 %all-gather.6.cloned.1.call-done = bf16[19200,128]{1,0:T(8,128)(2,1)} async-done(((bf16[600,128]{1,0:T(8,128)(2,1)}), bf16[19200,128]{1,0:T(8,128)(2,1)}) %all-gather.6.cloned.1.call-update) | async-done | bytes 4915216 | tf_op jit(solution)/shard_map/all_gather | solution.py:112
  77.9 7.6 %reshape.572 = bf16[8,4,76800]{2,1,0:T(4,128)(2,1)} reshape(bf16[19200,128]{1,0:T(8,128)(2,1)} %all-gather.6.cloned.1.call-done) | data formatting | bytes 9830400 | tf_op jit(solution)/shard_map/reshape | solution.py:57
  85.5 3.7 fusion.52
  97.1 4.5 reshape.581
  116.1 26.2 %all_gather.31 = bf16[1,512,640]{1,2,0:T(8,128)(2,1)S(1)} all-gather(bf16[1,128,640]{1,2,0:T(8,128)(2,1)S(1)} %pad_maximum_fusion.3), channel_id=1, replica_groups=mesh['dp'=8,'ctx'=4] {'ctx'}, dimensions={1}, use_global_device_ids=true | all-gather | bytes 819200 | tf_op jit(solution)/shard_map/all_gather | solution.py:150
  151.4 41.2 %all-gather.8.cloned.1.call-done = bf16[57600,128]{1,0:T(8,128)(2,1)} async-done(((bf16[1800,128]{1,0:T(8,128)(2,1)}), bf16[57600,128]{1,0:T(8,128)(2,1)}) %all-gather.8.cloned.1.call-update) | async-done | bytes 14745616 | tf_op jit(solution)/shard_map/all_gather | solution.py:113
  192.7 14.8 %reshape.582 = bf16[8,4,230400]{2,1,0:T(4,128)(2,1)} reshape(bf16[57600,128]{1,0:T(8,128)(2,1)} %all-gather.8.cloned.1.call-done) | data formatting | bytes 29491200 | tf_op jit(solution)/shard_map/reshape | solution.py:57
  207.4 13.3 %fusion.51 = (bf16[4,614400]{1,0:T(4,128)(2,1)}, bf16[4,614400]{1,0:T(4,128)(2,1)}, bf16[4,614400]{1,0:T(4,128)(2,1)}) fusion(bf16[4,1843200]{1,0:T(4,128)(2,1)} %bitcast.241), kind=kLoop, calls=%fused_computation.122 | loop fusion | bytes 29491200 | tf_op jit(solution)/shard_map/slice | solution.py:62
  220.7 9.6 %reshape.614 = bf16[2457600]{0:T(1024)(128)(2,1)} reshape(bf16[4,614400]{1,0:T(4,128)(2,1)} %get-tuple-element.12) | data formatting | bytes 9830400
  230.2 9.7 %reshape.586 = bf16[2560,960]{1,0:T(8,128)(2,1)} reshape(bf16[2457600]{0:T(1024)(128)(2,1)} %reshape.614) | data formatting | bytes 9830400 | tf_op jit(solution)/shard_map/reshape | solution.py:62
  239.9 9.2 %reshape.585 = bf16[960,2560]{1,0:T(8,128)(2,1)} reshape(bf16[4,614400]{1,0:T(4,128)(2,1)} %get-tuple-element.13) | data formatting | bytes 9830400 | tf_op jit(solution)/shard_map/reshape | solution.py:62
  249.1 9.2 %reshape.584 = bf16[960,2560]{1,0:T(8,128)(2,1)} reshape(bf16[4,614400]{1,0:T(4,128)(2,1)} %get-tuple-element.14) | data formatting | bytes 9830400 | tf_op jit(solution)/shard_map/reshape | solution.py:62
  264.5 3.7 multiply_convert_fusion
  268.2 4.1 fusion.60
  272.3 4.3 multiply_reduce_fusion
  284.9 3.7 copy.78
  293.6 31.8 %all_gather.39 = bf16[512,960]{0,1:T(8,128)(2,1)} all-gather(bf16[128,960]{0,1:T(8,128)(2,1)S(1)} %bitcast_convert_fusion), channel_id=1, replica_groups=mesh['dp'=8,'ctx'=4] {'ctx'}, dimensions={0}, use_global_device_ids=true | all-gather | bytes 1228800 | tf_op jit(solution)/shard_map/all_gather | solution.py:236
  329.4 49.0 %all_gather.36 = bf16[512,960]{0,1:T(8,128)(2,1)} all-gather(bf16[128,960]{0,1:T(8,128)(2,1)S(1)} %copy-done.20), channel_id=1, replica_groups=mesh['dp'=8,'ctx'=4] {'ctx'}, dimensions={0}, use_global_device_ids=true | all-gather | bytes 1228800 | tf_op jit(solution)/shard_map/all_gather | solution.py:233
  378.4 15.8 %all-to-all-start = ((bf16[128,4,240]{0,2,1:T(8,128)(2,1)}), bf16[128,4,240]{0,2,1:T(8,128)(2,1)S(1)}, u32[]{:S(2)}, u32[]{:S(2)}) async-start(bf16[128,4,240]{0,2,1:T(8,128)(2,1)} %multiply_convert_fusion.3), calls=%async_computation | async-start | bytes 491520 | tf_op jit(solution)/shard_map/all_to_all | solution.py:168
  404.0 5.1 all-to-all-start.3
  410.2 58.9 %all_gather.33 = bf16[512,960]{0,1:T(8,128)(2,1)S(1)} all-gather(bf16[128,960]{0,1:T(8,128)(2,1)S(1)} %bitcast.259), channel_id=1, replica_groups=mesh['dp'=8,'ctx'=4] {'ctx'}, dimensions={0}, use_global_device_ids=true | all-gather | bytes 1228800 | tf_op jit(solution)/shard_map/all_gather | solution.py:230
  472.7 12.6 %all-to-all-start.2 = ((bf16[128,4,240]{0,2,1:T(8,128)(2,1)}), bf16[128,4,240]{0,2,1:T(8,128)(2,1)S(1)}, u32[]{:S(2)}, u32[]{:S(2)}) async-start(bf16[128,4,240]{0,2,1:T(8,128)(2,1)} %bitcast.72), calls=%async_computation.2 | async-start | bytes 491520 | tf_op jit(solution)/shard_map/all_to_all | solution.py:170
  491.2 3.8 concatenate.68
  501.7 14.0 %all_gather.34 = bf16[512,320]{0,1:T(8,128)(2,1)S(1)} all-gather(bf16[128,320]{0,1:T(8,128)(2,1)S(1)} %bitcast.270), channel_id=1, replica_groups=mesh['dp'=8,'ctx'=4] {'ctx'}, dimensions={0}, use_global_device_ids=true | all-gather | bytes 409600 | tf_op jit(solution)/shard_map/all_gather | solution.py:231
  520.3 13.2 %all-gather = bf16[1,512,320]{1,2,0:T(8,128)(2,1)S(1)} all-gather(bf16[1,128,320]{1,2,0:T(8,128)(2,1)} %slice.122), channel_id=2, replica_groups=mesh['dp'=8,'ctx'=4] {'ctx'}, dimensions={1}, use_global_device_ids=true | all-gather | bytes 409600 | tf_op jit(solution)/shard_map/all_gather | solution.py:232
  542.5 3.7 convolution_convert_fusion.1
  546.2 3.8 concatenate.67
  550.0 3.7 concatenate.66
  553.7 6.0 pad_maximum_fusion
  559.8 5.3 fusion.9
  566.8 39.3 %psum.7 = f32[2,960]{1,0:T(2,128)S(1)} all-reduce(f32[2,960]{1,0:T(2,128)S(1)} %pad_maximum_fusion.7), channel_id=1, replica_groups=mesh['dp'=8,'ctx'=4] {'dp','ctx'}, use_global_device_ids=true, to_apply=%region_13.14 | all-reduce | flops 1920 | bytes 15360 | tf_op jit(solution)/shard_map/psum | solution.py:262
  609.3 18.5 %reduce-scatter.14.cloned.1.call-done = bf16[1800,128]{1,0:T(8,128)(2,1)} async-done(((bf16[14400,128]{1,0:T(8,128)(2,1)}), bf16[1800,128]{1,0:T(8,128)(2,1)}) %reduce-scatter.14.cloned.1.call-update) | async-done | bytes 460816
  (186 shorter events, 109.1 us)
Async XLA Ops:
  7.2 70.7 %all-gather.6.cloned.1.call-start = ((), (), s32[]{:S(2)}) async-start(), calls=%async_computation.7 | async-start | bytes 5068800 | tf_op jit(solution)/shard_map/all_gather | solution.py:112
  7.9 184.8 %all-gather.8.cloned.1.call-start = ((), (), s32[]{:S(2)}) async-start(), calls=%async_computation.8 | async-start | bytes 15206400 | tf_op jit(solution)/shard_map/all_gather | solution.py:113
  8.6 486.4 %reduce-scatter.10.cloned.1.call-start = ((), (), s32[]{:S(2)}) async-start(), calls=%async_computation.11 | async-start | bytes 819200
  10.4 75.1 %copy-start.33 = (f32[128]{0:T(128)}, f32[128]{0:T(128)S(1)}, u32[]{:S(2)}) copy-start(f32[128]{0:T(128)S(1)} %get-tuple-element.37) | copy-start | bytes 1540
  97.1 8.3 %copy-start.10 = (bf16[960,320]{1,0:T(8,128)(2,1)}, bf16[960,320]{1,0:T(8,128)(2,1)S(1)}, u32[]{:S(2)}) copy-start(bf16[960,320]{1,0:T(8,128)(2,1)S(1)} %reshape.574) | copy-start | bytes 1843204
  110.7 4.1 copy-start.12
  116.1 27.8 %copy-start.25 = (bf16[128,15,32]{0,2,1:T(8,128)(2,1)}, bf16[128,15,32]{0,2,1:T(8,128)(2,1)S(1)}, u32[]{:S(2)}) copy-start(bf16[128,15,32]{0,2,1:T(8,128)(2,1)S(1)} %get-tuple-element.26) | copy-start | bytes 368644
  116.1 27.8 %copy-start.27 = (bf16[128,15,32]{0,2,1:T(8,128)(2,1)}, bf16[128,15,32]{0,2,1:T(8,128)(2,1)S(1)}, u32[]{:S(2)}) copy-start(bf16[128,15,32]{0,2,1:T(8,128)(2,1)S(1)} %get-tuple-element.27) | copy-start | bytes 368644
  146.4 4.2 copy-start.32
  249.1 15.3 %slice-start = ((s8[5242880]{0:T(1024)(128)(4,1)}), s8[1048576]{0:T(1024)(128)(4,1)S(1)}, s32[]{:S(2)}) async-start(s8[5242880]{0:T(1024)(128)(4,1)} %bitcast.242), calls=%async_computation.14 | async-start | bytes 2097152
  258.3 6.1 slice-start.1
  272.3 4.4 copy-start.22
  272.3 4.4 copy-start.37
  272.3 6.1 copy-start.4
  284.9 6.6 %copy-start.31 = (f32[960]{0:T(1024)S(1)}, f32[960]{0:T(1024)}, u32[]{:S(2)}) copy-start(f32[960]{0:T(1024)} %param.11) | copy-start | bytes 11524
  284.9 7.8 %copy-start.34 = (f32[128]{0:T(128)S(1)}, f32[128]{0:T(128)}, u32[]{:S(2)}) copy-start(f32[128]{0:T(128)} %copy-done.33) | copy-start | bytes 1540
  290.9 38.5 %copy-start.20 = (bf16[128,960]{0,1:T(8,128)(2,1)S(1)}, bf16[128,960]{0,1:T(8,128)(2,1)}, u32[]{:S(2)}) copy-start(bf16[128,960]{0,1:T(8,128)(2,1)} %copy-done.19) | copy-start | bytes 737284
  290.9 248.0 %all-gather.12.cloned.1.call-start = ((), (), s32[]{:S(2)}) async-start(), calls=%async_computation.10 | async-start | bytes 3276800 | tf_op jit(solution)/shard_map/all_gather | solution.py:235
  325.4 53.0 %all-to-all-start.1 = ((bf16[128,4,240]{0,2,1:T(8,128)(2,1)}), bf16[128,4,240]{0,2,1:T(8,128)(2,1)S(1)}, u32[]{:S(2)}, u32[]{:S(2)}) async-start(bf16[128,4,240]{0,2,1:T(8,128)(2,1)} %bitcast.69), calls=%async_computation.1 | async-start | bytes 491520 | tf_op jit(solution)/shard_map/all_to_all | solution.py:169
  328.8 213.8 %all-gather.10.cloned.1.call-start = ((), (), s32[]{:S(2)}) async-start(), calls=%async_computation.9 | async-start | bytes 3276800 | tf_op jit(solution)/shard_map/all_gather | solution.py:234
  378.4 25.6 %all-to-all-start = ((bf16[128,4,240]{0,2,1:T(8,128)(2,1)}), bf16[128,4,240]{0,2,1:T(8,128)(2,1)S(1)}, u32[]{:S(2)}, u32[]{:S(2)}) async-start(bf16[128,4,240]{0,2,1:T(8,128)(2,1)} %multiply_convert_fusion.3), calls=%async_computation | async-start | bytes 491520 | tf_op jit(solution)/shard_map/all_to_all | solution.py:168
  404.0 68.8 %all-to-all-start.3 = ((bf16[128,4,640]{2,0,1:T(8,128)(2,1)}), bf16[128,4,640]{2,0,1:T(8,128)(2,1)}, u32[]{:S(2)}, u32[]{:S(2)}) async-start(bf16[128,4,640]{2,0,1:T(8,128)(2,1)} %bitcast.255), calls=%async_computation.3 | async-start | bytes 1310720 | tf_op jit(solution)/shard_map/all_to_all | solution.py:171
  410.2 62.5 %copy-start.17 = (bf16[128,15,64]{0,2,1:T(8,128)(2,1)}, bf16[128,15,64]{0,2,1:T(8,128)(2,1)S(1)}, u32[]{:S(2)}) copy-start(bf16[128,15,64]{0,2,1:T(8,128)(2,1)S(1)} %maximum_convert_fusion) | copy-start | bytes 737284
  472.7 66.2 %all-to-all-start.2 = ((bf16[128,4,240]{0,2,1:T(8,128)(2,1)}), bf16[128,4,240]{0,2,1:T(8,128)(2,1)S(1)}, u32[]{:S(2)}, u32[]{:S(2)}) async-start(bf16[128,4,240]{0,2,1:T(8,128)(2,1)} %bitcast.72), calls=%async_computation.2 | async-start | bytes 491520 | tf_op jit(solution)/shard_map/all_to_all | solution.py:170
  485.3 122.3 %reduce-scatter.12.cloned.1.call-start = ((), (), s32[]{:S(2)}) async-start(), calls=%async_computation.12 | async-start | bytes 1382400
  538.9 88.9 %reduce-scatter.14.cloned.1.call-start = ((), (), s32[]{:S(2)}) async-start(), calls=%async_computation.13 | async-start | bytes 4147200
  559.7 5.3 copy-start.13
  559.7 5.3 copy-start.24
  559.7 5.7 copy-start.11
  559.8 5.7 copy-start.30
  565.4 41.2 %copy-start.23 = (f32[128,960]{0,1:T(8,128)S(1)}, f32[128,960]{0,1:T(8,128)}, u32[]{:S(2)}) copy-start(f32[128,960]{0,1:T(8,128)} %get-tuple-element.11) | copy-start | bytes 1474564
  565.4 41.2 %copy-start.38 = (f32[128]{0:T(128)S(1)}, f32[128]{0:T(128)}, u32[]{:S(2)}) copy-start(f32[128]{0:T(128)} %get-tuple-element.36) | copy-start | bytes 1540
  (20 other events, 40.7 us)
Sparse Core Ops, SparseCore 0:
  10.8 66.9 all-gather.5
  80.7 111.8 all-gather.7
  291.1 28.9 reduce-scatter.9
  321.5 74.3 all-gather.11
  397.3 83.4 all-gather.9
  539.0 35.7 reduce-scatter.11
  578.3 49.4 reduce-scatter.13
where the time goes:
time: 646 us; the launch traced here: 637 us
  blocking collectives  232 us (36%)
  local copies, waits for them, and re-layouts  147 us (23%)
  waiting for transfers between devices  126 us (20%)
  matrix products  53.6 us (8%)
  starting transfers between devices  37.2 us (6%)
  other arithmetic  26 us (4%)
  between operations  15.2 us (2%)
    all_gather x1, waiting for transfers between devices, body(): lax.all_gather(attn_flat, ('dp', 'ctx'), axis=0, tiled=True)  63.6 us
    all_gather x1, blocking collectives, body(): lax.all_gather(grad_query, 'ctx', axis=0, tiled=True)  58.9 us
    all_gather x1, blocking collectives, body(): lax.all_gather(grad_mid_low, 'ctx', axis=0, tiled=True)  49 us
    all_gather x1, waiting for transfers between devices, body(): lax.all_gather(mlp_flat, ('dp', 'ctx'), axis=0, tiled=True)  41.2 us
    reshape x7, local copies, waits for them, and re-layouts, unpack_blocks(): pieces[:, offset:offset + length].reshape(height, width_cols)  40.4 us
    psum x1, blocking collectives, body(): lax.psum(jnp.stack([grad_gain_one, grad_gain_two]), ('dp', 'ctx'))  39.3 us
    all_gather x1, blocking collectives, body(): lax.all_gather(cot_low, 'ctx', axis=0, tiled=True)  31.8 us
    unnamed x89, local copies, waits for them, and re-layouts  31 us
  transfers between devices with their start and end apart: 11, of which 3 were waited for; matrix products, arithmetic and copies ran while one was open for 19% of the time, Pallas kernels for 0%

commit v1 on v0

--- a/solution.py
+++ b/solution.py
@@ -93,7 +93,7 @@
     )
 
 
-def body(hidden_in, segments, attn_flat, mlp_flat, norm_one, norm_two, cotangent):
+def body_rows(hidden_in, segments, attn_flat, mlp_flat, norm_one, norm_two, cotangent):
     seq_count, local_len, model_width = hidden_in.shape
     seq_len = segments.shape[1]
     row_count = seq_count * local_len
@@ -270,6 +270,357 @@
     )
 
 
+def gain_total(gain_rows):
+    total = gain_rows
+    for step in range(1, lax.axis_size("ctx")):
+        total = total + lax.ppermute(gain_rows, "ctx", swap_pairs("ctx", step))
+    step = 1
+    while step < lax.axis_size("dp"):
+        total = total + lax.ppermute(total, "dp", swap_pairs("dp", step))
+        step = 2 * step
+    return total
+
+
+def swap_pairs(axis, step):
+    return [(place, place ^ step) for place in range(lax.axis_size(axis))]
+
+
+def spread(rows):
+    return [rows] + [
+        lax.ppermute(rows, "ctx", swap_pairs("ctx", step)) for step in range(1, lax.axis_size("ctx"))
+    ]
+
+
+def collect(parts):
+    total = parts[0]
+    for step in range(1, lax.axis_size("ctx")):
+        moved = lax.ppermute(parts[step].astype(jnp.bfloat16), "ctx", swap_pairs("ctx", step))
+        total = total + moved.astype(jnp.float32)
+    return total
+
+
+def trade(blocks):
+    here = lax.axis_index("ctx")
+    got = [lax.dynamic_index_in_dim(blocks, here, 0, False)]
+    for step in range(1, lax.axis_size("ctx")):
+        block = lax.dynamic_index_in_dim(blocks, here ^ step, 0, False)
+        got.append(lax.ppermute(block, "ctx", swap_pairs("ctx", step)))
+    return got
+
+
+def in_order(pieces):
+    here = lax.axis_index("ctx")
+    step = 1
+    while step < len(pieces):
+        bit = (here & step) != 0
+        pieces = [
+            jnp.where(bit, pieces[place ^ step], pieces[place]) for place in range(len(pieces))
+        ]
+        step = 2 * step
+    return jnp.stack(pieces)
+
+
+def columns_apply(dp_count, ctx_count, rows):
+    unit = FFN // 128
+    return (
+        rows % unit == 0
+        and FFN % (128 * ctx_count) == 0
+        and D % ctx_count == 0
+        and ctx_count & (ctx_count - 1) == 0
+        and dp_count & (dp_count - 1) == 0
+        and rows % ctx_count == 0
+        and (2 * (D // ctx_count) % (rows // unit)) * unit % ctx_count == 0
+        and (rows - (2 * (D // ctx_count) % (rows // unit)) * unit) % ctx_count == 0
+    )
+
+
+def mlp_sizes(rows, ctx_count):
+    unit = FFN // 128
+    held = rows // unit
+    tall = 2 * (D // ctx_count)
+    return unit, unit // ctx_count, held, tall // held, tall % held
+
+
+def gather_mlp(flat):
+    ctx_count = lax.axis_size("ctx")
+    place = lax.axis_index("dp")
+    rows = flat.shape[0]
+    unit, part, held, edge, rest = mlp_sizes(rows, ctx_count)
+    cut = rest * unit
+
+    def by_column(block, count):
+        return (
+            block.reshape(count, ctx_count, part, 128)
+            .transpose(1, 0, 2, 3)
+            .reshape(ctx_count, count * part, 128)
+        )
+
+    full = by_column(flat, held)
+    tail = flat[cut:].reshape(ctx_count, -1, 128)
+    mixed = jnp.concatenate([by_column(flat[:cut], rest), tail], axis=1)
+    got = in_order(trade(jnp.where(place < edge, full, mixed)))
+    kept = jnp.concatenate([got[:, : rest * part], tail], axis=1)
+    block = jnp.where(
+        place < edge, got, jnp.where(place == edge, kept, flat.reshape(ctx_count, -1, 128))
+    )
+    whole = lax.all_gather(block.reshape(rows, 128), "dp", axis=0, tiled=True)
+    whole = whole.reshape(-1, ctx_count, rows // ctx_count, 128)
+    tall = jnp.concatenate(
+        [
+            whole[:edge]
+            .reshape(edge, ctx_count, held, part, 128)
+            .transpose(1, 0, 2, 3, 4)
+            .reshape(ctx_count, edge * held, part * 128),
+            whole[edge, :, : rest * part].reshape(ctx_count, rest, part * 128),
+        ],
+        axis=1,
+    )
+    half = tall.shape[1] // 2
+    w_gate = tall[:, :half].reshape(D, part * 128)
+    w_up = tall[:, half:].reshape(D, part * 128)
+    w_down = jnp.concatenate(
+        [whole[edge, :, rest * part :].reshape(-1, 128), whole[edge + 1 :].reshape(-1, 128)], axis=0
+    ).reshape(FFN // ctx_count, D)
+    return w_gate, w_up, w_down
+
+
+def scatter_mlp(grad_w_gate, grad_w_up, grad_w_down, rows):
+    ctx_count = lax.axis_size("ctx")
+    place = lax.axis_index("dp")
+    unit, part, held, edge, rest = mlp_sizes(rows, ctx_count)
+    low = jnp.bfloat16
+    tall = jnp.concatenate(
+        [
+            grad_w_gate.astype(low).reshape(ctx_count, -1, part, 128),
+            grad_w_up.astype(low).reshape(ctx_count, -1, part, 128),
+        ],
+        axis=1,
+    )
+    down = grad_w_down.astype(low).reshape(-1, 128)
+    first = (
+        tall[:, : edge * held]
+        .reshape(ctx_count, edge, held * part, 128)
+        .transpose(1, 0, 2, 3)
+        .reshape(edge * rows, 128)
+    )
+    cut = rest * unit
+    middle = jnp.concatenate(
+        [
+            tall[:, edge * held :].reshape(ctx_count, rest * part, 128),
+            down[: rows - cut].reshape(ctx_count, -1, 128),
+        ],
+        axis=1,
+    ).reshape(rows, 128)
+    terms = jnp.concatenate([first, middle, down[rows - cut :]], axis=0)
+    own = lax.psum_scatter(terms, "dp", scatter_dimension=0, tiled=True)
+    blocks = own.reshape(ctx_count, rows // ctx_count, 128)
+    got = in_order(trade(blocks))
+
+    def by_row(block, count):
+        return block.reshape(ctx_count, count, part, 128).transpose(1, 0, 2, 3).reshape(-1, 128)
+
+    full = by_row(got, held)
+    mixed = jnp.concatenate(
+        [by_row(got[:, : rest * part], rest), blocks[:, rest * part :].reshape(-1, 128)], axis=0
+    )
+    out = jnp.where(place < edge, full, jnp.where(place == edge, mixed, own))
+    return out.astype(jnp.float32)
+
+
+def body(hidden_in, segments, attn_flat, mlp_flat, norm_one, norm_two, cotangent):
+    if not columns_apply(lax.axis_size("dp"), lax.axis_size("ctx"), mlp_flat.shape[0]):
+        return body_rows(hidden_in, segments, attn_flat, mlp_flat, norm_one, norm_two, cotangent)
+    return body_columns(hidden_in, segments, attn_flat, mlp_flat, norm_one, norm_two, cotangent)
+
+
+def body_columns(hidden_in, segments, attn_flat, mlp_flat, norm_one, norm_two, cotangent):
+    seq_count, local_len, model_width = hidden_in.shape
+    seq_len = segments.shape[1]
+    row_count = seq_count * local_len
+    groups = HEADS // KV_HEADS
+    qwidth = HEADS * HEAD_DIM
+    kwidth = KV_HEADS * HEAD_DIM
+    score_scale = HEAD_DIM ** (-0.5)
+    low = jnp.bfloat16
+    wide = jnp.float32
+    dp_count = lax.axis_size("dp")
+    ctx_count = lax.axis_size("ctx")
+    here = lax.axis_index("ctx")
+    attn_shapes = ((D, qwidth), (D, kwidth), (D, kwidth), (qwidth, D))
+    back = -(-(seq_len // 2 - 1) // local_len)
+    start_row = here * local_len
+
+    attn_near = in_order(spread(attn_flat)).reshape(-1, 128)
+    attn_whole = lax.all_gather(attn_near, "dp", axis=0, tiled=True)
+    w_query, w_key, w_value, w_out = unpack_blocks(attn_whole, attn_shapes, dp_count, ctx_count)
+    w_gate, w_up, w_down = gather_mlp(mlp_flat)
+
+    pos_all = positions_of(segments)
+    pos_local = lax.dynamic_slice_in_dim(pos_all, start_row, local_len, 1)
+    seg_local = lax.dynamic_slice_in_dim(segments, start_row, local_len, 1)
+    seg_near = lax.dynamic_slice_in_dim(
+        jnp.pad(segments, ((0, 0), (back * local_len, 0)), constant_values=-1),
+        start_row,
+        (back + 1) * local_len,
+        1,
+    )
+    cosine_table, sine_table = rope_tables(pos_local.reshape(-1))
+    key_index = jnp.arange((back + 1) * local_len, dtype=jnp.int32) - back * local_len
+    query_index = jnp.arange(local_len, dtype=jnp.int32)
+    allowed = (seg_local[:, :, None] == seg_near[:, None, :]) & (
+        key_index[None, None, :] <= query_index[None, :, None]
+    )
+    allowed = allowed[:, None, None]
+
+    residual = hidden_in.reshape(row_count, model_width)
+    cot_rows = cotangent.reshape(row_count, model_width)
+    cot_low = cot_rows.astype(low)
+    cot_all = jnp.concatenate(spread(cot_low), axis=0)
+    inv_one, normed_one = norm_forward(residual, norm_one)
+    normed_one = normed_one.astype(low)
+
+    def cols(rows):
+        blocks = rows.reshape(row_count, ctx_count, -1).transpose(1, 0, 2)
+        return jnp.concatenate(trade(blocks), axis=0)
+
+    one_cols = cols(normed_one)
+    query = jnp.dot(normed_one, w_query, preferred_element_type=wide).reshape(
+        row_count, HEADS, HEAD_DIM
+    )
+    key_raw = jnp.dot(normed_one, w_key, preferred_element_type=wide).reshape(
+        row_count, KV_HEADS, HEAD_DIM
+    )
+    value_low = jnp.dot(normed_one, w_value, preferred_element_type=wide).astype(low)
+    key_rot = rotate(key_raw, cosine_table, sine_table).astype(low)
+    kv_local = jnp.concatenate(
+        [
+            key_rot.reshape(seq_count, local_len, kwidth),
+            value_low.reshape(seq_count, local_len, kwidth),
+        ],
+        axis=2,
+    )
+    up_pairs = [
+        [(place, place + step) for place in range(ctx_count - step)] for step in range(back + 1)
+    ]
+    down_pairs = [[(right, left) for left, right in pairs] for pairs in up_pairs]
+    kv_near = jnp.concatenate(
+        [lax.ppermute(kv_local, "ctx", up_pairs[step]) for step in range(back, 0, -1)] + [kv_local],
+        axis=1,
+    )
+    query_rot = (
+        rotate(query, cosine_table, sine_table)
+        .astype(low)
+        .reshape(seq_count, local_len, KV_HEADS, groups, HEAD_DIM)
+    )
+    near_len = (back + 1) * local_len
+    key_near = kv_near[:, :, :kwidth].reshape(seq_count, near_len, KV_HEADS, HEAD_DIM)
+    value_near = kv_near[:, :, kwidth:].reshape(seq_count, near_len, KV_HEADS, HEAD_DIM)
+    scores = masked_scores(query_rot, key_near, allowed, score_scale)
+    row_top = jnp.max(scores, axis=-1, keepdims=True)
+    log_total = row_top + jnp.log(jnp.sum(jnp.exp(scores - row_top), axis=-1, keepdims=True))
+    attn_probs = jnp.exp(scores - log_total)
+    probs_low = attn_probs.astype(low)
+    head_mix = jnp.einsum("skgql,slkd->sqkgd", probs_low, value_near, preferred_element_type=wide)
+    head_mix = head_mix.reshape(row_count, qwidth).astype(low)
+    middle = residual + jnp.dot(head_mix, w_out, preferred_element_type=wide)
+    inv_two, normed_two = norm_forward(middle, norm_two)
+    two_all = jnp.concatenate(spread(normed_two.astype(low)), axis=0)
+    mix_cols = cols(head_mix)
+
+    grad_active = jnp.dot(cot_all, w_down.T, preferred_element_type=wide)
+    gate_pre = jnp.dot(two_all, w_gate, preferred_element_type=wide)
+    up_proj = jnp.dot(two_all, w_up, preferred_element_type=wide)
+    gate_sigmoid = jax.nn.sigmoid(gate_pre)
+    active = (gate_pre * gate_sigmoid * up_proj).astype(low)
+    grad_gate = (
+        grad_active * up_proj * gate_sigmoid * (1.0 + gate_pre * (1.0 - gate_sigmoid))
+    ).astype(low)
+    grad_up = (grad_active * gate_pre * gate_sigmoid).astype(low)
+    two_terms = jnp.dot(grad_gate, w_gate.T, preferred_element_type=wide) + jnp.dot(
+        grad_up, w_up.T, preferred_element_type=wide
+    )
+    grad_normed_two = collect(jnp.split(two_terms, ctx_count, axis=0))
+    block_terms = jnp.dot(active, w_down, preferred_element_type=wide)
+    block_rows = middle + collect(jnp.split(block_terms, ctx_count, axis=0))
+    mlp_grad = scatter_mlp(
+        left_dot(two_all, grad_gate),
+        left_dot(two_all, grad_up),
+        left_dot(active, cot_all),
+        mlp_flat.shape[0],
+    )
+
+    grad_middle, grad_gain_two = norm_backward(middle, inv_two, norm_two, grad_normed_two)
+    grad_middle = cot_rows + grad_middle
+    grad_mid_low = grad_middle.astype(low)
+    mid_all = jnp.concatenate(spread(grad_mid_low), axis=0)
+    grad_mix = jnp.dot(grad_mid_low, w_out.T, preferred_element_type=wide).astype(low)
+    grad_mix = grad_mix.reshape(seq_count, local_len, KV_HEADS, groups, HEAD_DIM)
+    grad_probs = jnp.einsum("sqkgd,slkd->skgql", grad_mix, value_near, preferred_element_type=wide)
+    grad_value_near = jnp.einsum(
+        "skgql,sqkgd->slkd", probs_low, grad_mix, preferred_element_type=wide
+    )
+    grad_scores = attn_probs * (
+        grad_probs - jnp.sum(attn_probs * grad_probs, axis=-1, keepdims=True)
+    )
+    grad_scores_low = (grad_scores * score_scale).astype(low)
+    grad_query = jnp.einsum(
+        "skgql,slkd->sqkgd", grad_scores_low, key_near, preferred_element_type=wide
+    )
+    grad_key_near = jnp.einsum(
+        "skgql,sqkgd->slkd", grad_scores_low, query_rot, preferred_element_type=wide
+    )
+    kv_terms = jnp.concatenate(
+        [
+            grad_key_near.reshape(seq_count, near_len, kwidth),
+            grad_value_near.reshape(seq_count, near_len, kwidth),
+        ],
+        axis=2,
+    )
+    kv_owned = kv_terms[:, back * local_len :]
+    for step in range(1, back + 1):
+        first = (back - step) * local_len
+        moved = lax.ppermute(
+            kv_terms[:, first : first + local_len].astype(low), "ctx", down_pairs[step]
+        )
+        kv_owned = kv_owned + moved.astype(wide)
+    grad_key = kv_owned[:, :, :kwidth].reshape(row_count, KV_HEADS, HEAD_DIM)
+    grad_value = kv_owned[:, :, kwidth:].reshape(row_count, kwidth).astype(low)
+    grad_query = (
+        unrotate(grad_query.reshape(row_count, HEADS, HEAD_DIM), cosine_table, sine_table)
+        .reshape(row_count, qwidth)
+        .astype(low)
+    )
+    grad_key = unrotate(grad_key, cosine_table, sine_table).reshape(row_count, kwidth).astype(low)
+    grad_kv = jnp.concatenate([grad_key, grad_value], axis=1)
+    all_query = jnp.concatenate(spread(grad_query), axis=0)
+    all_kv = jnp.concatenate(spread(grad_kv), axis=0)
+    attn_terms = jnp.concatenate(
+        [
+            left_dot(one_cols, all_query).astype(low).reshape(-1),
+            left_dot(one_cols, all_kv[:, :kwidth]).astype(low).reshape(-1),
+            left_dot(one_cols, all_kv[:, kwidth:]).astype(low).reshape(-1),
+            left_dot(mix_cols, mid_all).astype(low).reshape(-1),
+        ]
+    ).reshape(-1, 128)
+    attn_grad = lax.psum_scatter(attn_terms, "dp", scatter_dimension=0, tiled=True).astype(wide)
+    grad_normed_one = (
+        jnp.dot(grad_query, w_query.T, preferred_element_type=wide)
+        + jnp.dot(grad_key, w_key.T, preferred_element_type=wide)
+        + jnp.dot(grad_value, w_value.T, preferred_element_type=wide)
+    )
+    grad_resid, grad_gain_one = norm_backward(residual, inv_one, norm_one, grad_normed_one)
+    grad_resid = grad_middle + grad_resid
+    gain_sums = gain_total(jnp.stack([grad_gain_one, grad_gain_two]))
+    return (
+        block_rows.reshape(seq_count, local_len, model_width),
+        grad_resid.reshape(seq_count, local_len, model_width),
+        attn_grad,
+        mlp_grad,
+        gain_sums[0],
+        gain_sums[1],
+    )
+
+
 def solution(mesh):
     in_specs = (
         P("dp", "ctx", None),

time: 646 us -> 442 us (0.68)
  blocking collectives: 232 us -> 0 us
  starting transfers between devices: 37.2 us -> 86.5 us
  local copies, waits for them, and re-layouts: 147 us -> 132 us
  matrix products: 53.6 us -> 43.8 us
  other arithmetic: 26 us -> 33.4 us
    all_gather x6 -> x0, blocking collectives: 193 us -> none  [the longest x1 58.9 us: body(): lax.all_gather(grad_query, 'ctx', axis=0, tiled=True)]
    ppermute x0 -> x46, starting transfers between devices: none -> 86.3 us  [the longest x18 43.7 us: spread(): lax.ppermute(rows, 'ctx', swap_pairs('ctx', step))]
    ppermute x0 -> x46, waiting for transfers between devices: none -> 84.8 us  [the longest x18 26.7 us: spread(): lax.ppermute(rows, 'ctx', swap_pairs('ctx', step))]
    all_gather x4 -> x2, waiting for transfers between devices: 105 us -> 29 us  [the longest x1 16.2 us: body_columns(): attn_whole = lax.all_gather(attn_near, 'dp', axis=0, tiled=True)]
    psum x1 -> x0, blocking collectives: 39.3 us -> none  [body(): lax.psum(jnp.stack([grad_gain_one, grad_gain_two]), ('dp', 'ctx'))]
    all_to_all x4 -> x0, starting transfers between devices: 37 us -> none  [the longest x1 15.8 us: body(): lax.all_to_all(normed_one, 'ctx', split_axis=1, concat_axis=0, tiled=True)]
    reshape x4 -> x22, local copies, waits for them, and re-layouts: 7.54 us -> 40.1 us  [the longest x2 8.7 us: gather_mlp(): tall = jnp.concatenate([whole[:edge].reshape(edge, ctx_count, held, part,...]
    reshape x7 -> x4, local copies, waits for them, and re-layouts: 40.4 us -> 12 us  [unpack_blocks(): pieces[:, offset:offset + length].reshape(height, width_cols)]
  transfers between devices with their start and end apart: 11 -> 50, of which waited for: 3 -> 23; matrix products, arithmetic and copies ran while one was open for 19% -> 45% of each run, Pallas kernels for 0% -> 0%
where the time goes in v1:
time: 442 us; the launch traced here: 435 us
  local copies, waits for them, and re-layouts  132 us (30%)
  waiting for transfers between devices  124 us (28%)
  starting transfers between devices  86.5 us (20%)
  matrix products  43.8 us (10%)
  other arithmetic  33.4 us (8%)
  between operations  15.5 us (4%)
    ppermute x18, starting transfers between devices, spread(): lax.ppermute(rows, 'ctx', swap_pairs('ctx', step))  43.7 us
    ppermute x18, waiting for transfers between devices, spread(): lax.ppermute(rows, 'ctx', swap_pairs('ctx', step))  26.7 us
    ppermute x2, waiting for transfers between devices, body_columns(): lax.ppermute(kv_terms[:, first:first + local_len].astype(low), 'ctx', dow...  17.9 us
    ppermute x12, waiting for transfers between devices, trade(): got.append(lax.ppermute(block, 'ctx', swap_pairs('ctx', step)))  16.7 us
    ppermute x6, waiting for transfers between devices, collect(): lax.ppermute(parts[step].astype(jnp.bfloat16), 'ctx', swap_pairs('ctx', s...  16.6 us
    ppermute x12, starting transfers between devices, trade(): got.append(lax.ppermute(block, 'ctx', swap_pairs('ctx', step)))  16.5 us
    all_gather x1, waiting for transfers between devices, body_columns(): attn_whole = lax.all_gather(attn_near, 'dp', axis=0, tiled=True)  16.2 us
    unnamed x104, local copies, waits for them, and re-layouts  13.5 us
  transfers between devices with their start and end apart: 50, of which 23 were waited for; matrix products, arithmetic and copies ran while one was open for 45% of the time, Pallas kernels for 0%

profile of v1, /device:TPU:0, one launch (start us, length us, event | category | flops | bytes accessed | tf_op | source)
XLA Modules:
  0.0 435.5 jit_solution(15474146438838610154)
XLA Ops:
  10.6 5.1 %collective-permute-start.8 = (bf16[450,128]{1,0:T(8,128)(2,1)S(1)}, bf16[450,128]{1,0:T(8,128)(2,1)S(1)}, u32[]{:S(2)}, u32[]{:S(2)}) collective-permute-start(bf16[450,128]{1,0:T(8,128)(2,1)S(1)} %bitcast.313), channel_id=1, source_target_pairs={{0,3},{1,2},{2,1},{3,0},{4,7},{5,6},{6,5},{7,4},{8,11},{9,10},{10,... | collective-permute-start | bytes 345608 | tf_op jit(solution)/shard_map/ppermute | solution.py:307
  19.8 5.7 %collective-permute-done.9 = bf16[450,128]{1,0:T(8,128)(2,1)S(1)} collective-permute-done((bf16[450,128]{1,0:T(8,128)(2,1)S(1)}, bf16[450,128]{1,0:T(8,128)(2,1)S(1)}, u32[]{:S(2)}, u32[]{:S(2)}) %collective-permute-start.9) | collective-permute-done | bytes 115232 | tf_op jit(solution)/shard_map/ppermute | solution.py:307
  31.3 8.8 %collective-permute-done.1 = bf16[600,128]{1,0:T(8,128)(2,1)S(1)} collective-permute-done((bf16[600,128]{1,0:T(8,128)(2,1)S(1)}, bf16[600,128]{1,0:T(8,128)(2,1)S(1)}, u32[]{:S(2)}, u32[]{:S(2)}) %collective-permute-start.1) | collective-permute-done | bytes 153632 | tf_op jit(solution)/shard_map/ppermute | solution.py:290
  49.7 12.8 %all-gather.5.cloned.1.call-done = bf16[14400,128]{1,0:T(8,128)(2,1)} async-done(((bf16[1800,128]{1,0:T(8,128)(2,1)}), bf16[14400,128]{1,0:T(8,128)(2,1)}) %all-gather.5.cloned.1.call-update) | async-done | bytes 3686416 | tf_op jit(solution)/shard_map/all_gather | solution.py:366
  62.5 5.0 %reshape.629 = bf16[8,4,450,128]{3,2,1,0:T(8,128)(2,1)} reshape(bf16[14400,128]{1,0:T(8,128)(2,1)} %all-gather.5.cloned.1.call-done) | data formatting | bytes 7372800 | tf_op jit(solution)/shard_map/reshape | solution.py:367
  76.1 4.5 %copy.103 = bf16[4,5,90,5,128]{4,3,2,1,0:T(8,128)(2,1)} copy(bf16[4,5,90,5,128]{4,3,2,0,1:T(8,128)(2,1)} %bitcast.266) | data formatting | bytes 4608000 | tf_op jit(solution)/shard_map/transpose | solution.py:372
  80.6 5.6 %reshape.627 = bf16[4,450,640]{2,1,0:T(8,128)(2,1)} reshape(bf16[4,5,90,5,128]{4,3,2,1,0:T(8,128)(2,1)} %copy.103) | data formatting | bytes 4608000 | tf_op jit(solution)/shard_map/reshape | solution.py:373
  88.5 16.2 %all-gather.3.cloned.1.call-done = bf16[19200,128]{1,0:T(8,128)(2,1)} async-done(((bf16[2400,128]{1,0:T(8,128)(2,1)}), bf16[19200,128]{1,0:T(8,128)(2,1)}) %all-gather.3.cloned.1.call-update) | async-done | bytes 4915216 | tf_op jit(solution)/shard_map/all_gather | solution.py:454
  104.8 7.6 %reshape.611 = bf16[8,4,76800]{2,1,0:T(4,128)(2,1)} reshape(bf16[19200,128]{1,0:T(8,128)(2,1)} %all-gather.3.cloned.1.call-done) | data formatting | bytes 9830400 | tf_op jit(solution)/shard_map/reshape | solution.py:57
  112.4 3.8 copy.147
  116.2 3.8 copy.132
  135.6 4.7 %collective-permute-start.3 = (bf16[1,128,640]{1,2,0:T(8,128)(2,1)S(1)}, bf16[1,128,640]{1,2,0:T(8,128)(2,1)S(1)}, u32[]{:S(2)}, u32[]{:S(2)}) collective-permute-start(bf16[1,128,640]{1,2,0:T(8,128)(2,1)S(1)} %pad_maximum_fusion.16), channel_id=1, source_target_pairs={{0,2},{1,3},{4,6},{5,7},{8,10},{9,11},{12,14},{13,15},{16,18},{17,... | collective-permute-start | bytes 491528 | tf_op jit(solution)/shard_map/ppermute | solution.py:507
  143.9 4.3 reshape.620
  176.0 7.7 %collective-permute-start.14 = (bf16[128,960]{0,1:T(8,128)(2,1)}, bf16[128,960]{0,1:T(8,128)(2,1)S(1)}, u32[]{:S(2)}, u32[]{:S(2)}) collective-permute-start(bf16[128,960]{0,1:T(8,128)(2,1)} %bitcast_convert_fusion), channel_id=1, source_target_pairs={{0,1},{1,0},{2,3},{3,2},{4,5},{5,4},{6,7},{7,6},{8,9},{9,8},{10,11... | collective-permute-start | bytes 737288 | tf_op jit(solution)/shard_map/ppermute | solution.py:290
  183.6 3.8 collective-permute-done.6
  230.1 4.7 %reshape.647 = bf16[4,240,5,128]{1,0,3,2:T(4,128)(2,1)} reshape(bf16[960,640]{0,1:T(8,128)(2,1)} %copy.109) | data formatting | bytes 2457600 | tf_op jit(solution)/shard_map/reshape | solution.py:394
  240.8 4.5 %reshape.648 = bf16[4,240,5,128]{1,0,3,2:T(4,128)(2,1)} reshape(bf16[960,640]{0,1:T(8,128)(2,1)} %copy.110) | data formatting | bytes 2457600 | tf_op jit(solution)/shard_map/reshape | solution.py:395
  249.9 5.3 %pad_maximum_fusion.1 = bf16[4,450,5,128]{1,0,3,2:T(4,128)(2,1)} fusion(bf16[4,240,5,128]{1,0,3,2:T(4,128)(2,1)} %reshape.648, bf16[4,240,5,128]{1,0,3,2:T(4,128)(2,1)} %reshape.647), kind=kLoop, calls=%fused_computation.11 | loop fusion | flops 4608000 | bytes 4761600 | tf_op jit(solution)/shard_map/concatenate | solution.py:392
  255.2 6.9 %copy.111 = bf16[4,450,5,128]{3,0,2,1:T(4,128)(2,1)} copy(bf16[4,450,5,128]{1,0,3,2:T(4,128)(2,1)} %pad_maximum_fusion.1) | data formatting | bytes 4608000 | tf_op jit(solution)/shard_map/slice | solution.py:401
  270.2 3.7 reshape.650
  273.9 5.6 %pad_maximum_fusion = bf16[14400,128]{1,0:T(8,128)(2,1)} fusion(bf16[3600,128]{1,0:T(8,128)(2,1)} %slice.156, bf16[1800,128]{1,0:T(8,128)(2,1)} %reshape.653, bf16[9000,128]{1,0:T(8,128)(2,1)} %reshape.650), kind=kLoop, calls=%fused_computation.1 | loop fusion | flops 11059200 | bytes 7372800 | tf_op jit(solution)/shard_map/concatenate | solution.py:414
  288.1 5.0 %collective-permute-done.11 = bf16[128,960]{0,1:T(8,128)(2,1)S(1)} collective-permute-done((bf16[128,960]{0,1:T(8,128)(2,1)S(1)}, bf16[128,960]{0,1:T(8,128)(2,1)S(1)}, u32[]{:S(2)}, u32[]{:S(2)}) %collective-permute-start.11) | collective-permute-done | bytes 245792 | tf_op jit(solution)/shard_map/ppermute | solution.py:297
  293.1 4.3 collective-permute-done.13
  297.4 7.3 %collective-permute-done.12 = bf16[128,960]{0,1:T(8,128)(2,1)S(1)} collective-permute-done((bf16[128,960]{0,1:T(8,128)(2,1)S(1)}, bf16[128,960]{0,1:T(8,128)(2,1)S(1)}, u32[]{:S(2)}, u32[]{:S(2)}) %collective-permute-start.12) | collective-permute-done | bytes 245792 | tf_op jit(solution)/shard_map/ppermute | solution.py:297
  314.7 4.4 %collective-permute-done.20 = bf16[1,128,640]{1,2,0:T(8,128)(2,1)S(1)} collective-permute-done((bf16[1,128,640]{1,2,0:T(8,128)(2,1)S(1)}, bf16[1,128,640]{1,2,0:T(8,128)(2,1)S(1)}, u32[]{:S(2)}, u32[]{:S(2)}) %collective-permute-start.20) | collective-permute-done | bytes 163872 | tf_op jit(solution)/shard_map/ppermute | solution.py:582
  320.4 13.5 %collective-permute-done.21 = bf16[1,128,640]{1,2,0:T(8,128)(2,1)S(1)} collective-permute-done((bf16[1,128,640]{1,2,0:T(8,128)(2,1)S(1)}, bf16[1,128,640]{1,2,0:T(8,128)(2,1)S(1)}, u32[]{:S(2)}, u32[]{:S(2)}) %collective-permute-start.21) | collective-permute-done | bytes 163872 | tf_op jit(solution)/shard_map/ppermute | solution.py:582
  339.1 7.6 %collective-permute-done.32 = bf16[128,240]{0,1:T(8,128)(2,1)S(1)} collective-permute-done((bf16[128,240]{0,1:T(8,128)(2,1)}, bf16[128,240]{0,1:T(8,128)(2,1)S(1)}, u32[]{:S(2)}, u32[]{:S(2)}) %collective-permute-start.32) | collective-permute-done | bytes 61472 | tf_op jit(solution)/shard_map/ppermute | solution.py:307
  346.8 16.8 %collective-permute-start.25 = (bf16[128,960]{0,1:T(8,128)(2,1)S(1)}, bf16[128,960]{0,1:T(8,128)(2,1)}, u32[]{:S(2)}, u32[]{:S(2)}) collective-permute-start(bf16[128,960]{0,1:T(8,128)(2,1)S(1)} %bitcast.303), channel_id=1, source_target_pairs={{0,1},{1,0},{2,3},{3,2},{4,5},{5,4},{6,7},{7,6},{8,9},{9,8},{10,11... | collective-permute-start | bytes 737288 | tf_op jit(solution)/shard_map/ppermute | solution.py:290
  363.6 4.8 %collective-permute-done.35 = bf16[128,960]{0,1:T(8,128)(2,1)S(1)} collective-permute-done((bf16[128,960]{0,1:T(8,128)(2,1)S(1)}, bf16[128,960]{0,1:T(8,128)(2,1)S(1)}, u32[]{:S(2)}, u32[]{:S(2)}) %collective-permute-start.35) | collective-permute-done | bytes 245792 | tf_op jit(solution)/shard_map/ppermute | solution.py:290
  368.4 5.7 %collective-permute-start.28 = (bf16[128,640]{0,1:T(8,128)(2,1)S(1)}, bf16[128,640]{0,1:T(8,128)(2,1)S(1)}, u32[]{:S(2)}, u32[]{:S(2)}) collective-permute-start(bf16[128,640]{0,1:T(8,128)(2,1)S(1)} %pad_maximum_fusion.17), channel_id=1, source_target_pairs={{0,1},{1,0},{2,3},{3,2},{4,5},{5,4},{6,7},{7,6},{8,9},{9,8},{10,11... | collective-permute-start | bytes 491528 | tf_op jit(solution)/shard_map/ppermute | solution.py:290
  375.3 6.8 %collective-permute-done.26 = bf16[128,960]{0,1:T(8,128)(2,1)} collective-permute-done((bf16[128,960]{0,1:T(8,128)(2,1)S(1)}, bf16[128,960]{0,1:T(8,128)(2,1)}, u32[]{:S(2)}, u32[]{:S(2)}) %collective-permute-start.26) | collective-permute-done | bytes 245792 | tf_op jit(solution)/shard_map/ppermute | solution.py:290
  414.1 9.9 %reduce-scatter.7.cloned.1.call-done = bf16[600,128]{1,0:T(8,128)(2,1)} async-done(((bf16[4800,128]{1,0:T(8,128)(2,1)}), bf16[600,128]{1,0:T(8,128)(2,1)}) %reduce-scatter.7.cloned.1.call-update) | async-done | bytes 153616
  (344 shorter events, 203.7 us)
Async XLA Ops:
  7.2 55.3 %all-gather.5.cloned.1.call-start = ((), (), s32[]{:S(2)}) async-start(), calls=%async_computation.3 | async-start | bytes 4147200 | tf_op jit(solution)/shard_map/all_gather | solution.py:366
  27.7 77.1 %all-gather.3.cloned.1.call-start = ((), (), s32[]{:S(2)}) async-start(), calls=%async_computation.2 | async-start | bytes 5529600 | tf_op jit(solution)/shard_map/all_gather | solution.py:454
  42.5 365.3 %reduce-scatter.9.cloned.1.call-start = ((), (), s32[]{:S(2)}) async-start(), calls=%async_computation.5 | async-start | bytes 4147200
  43.3 150.9 %collective-permute-start.16 = (bf16[128,960]{0,1:T(8,128)(2,1)}, bf16[128,960]{0,1:T(8,128)(2,1)}, u32[]{:S(2)}, u32[]{:S(2)}) collective-permute-start(bf16[128,960]{0,1:T(8,128)(2,1)} %bitcast_convert_fusion), channel_id=1, source_target_pairs={{0,3},{1,2},{2,1},{3,0},{4,7},{5,6},{6,5},{7,4},{8,11},{9,10},{10,... | collective-permute-start | bytes 737288 | tf_op jit(solution)/shard_map/ppermute | solution.py:290
  44.9 149.3 %collective-permute-start.15 = (bf16[128,960]{0,1:T(8,128)(2,1)}, bf16[128,960]{0,1:T(8,128)(2,1)}, u32[]{:S(2)}, u32[]{:S(2)}) collective-permute-start(bf16[128,960]{0,1:T(8,128)(2,1)} %bitcast_convert_fusion), channel_id=1, source_target_pairs={{0,2},{1,3},{2,0},{3,1},{4,6},{5,7},{6,4},{7,5},{8,10},{9,11},{10,... | collective-permute-start | bytes 737288 | tf_op jit(solution)/shard_map/ppermute | solution.py:290
  132.2 26.3 %collective-permute-start.4 = (bf16[1,128,640]{1,2,0:T(8,128)(2,1)S(1)}, bf16[1,128,640]{1,2,0:T(8,128)(2,1)S(1)}, u32[]{:S(2)}, u32[]{:S(2)}) collective-permute-start(bf16[1,128,640]{1,2,0:T(8,128)(2,1)S(1)} %pad_maximum_fusion.16), channel_id=1, source_target_pairs={{0,1},{1,2},{2,3},{4,5},{5,6},{6,7},{8,9},{9,10},{10,11},{12,13},{... | collective-permute-start | bytes 491528 | tf_op jit(solution)/shard_map/ppermute | solution.py:507
  135.6 22.9 %collective-permute-start.3 = (bf16[1,128,640]{1,2,0:T(8,128)(2,1)S(1)}, bf16[1,128,640]{1,2,0:T(8,128)(2,1)S(1)}, u32[]{:S(2)}, u32[]{:S(2)}) collective-permute-start(bf16[1,128,640]{1,2,0:T(8,128)(2,1)S(1)} %pad_maximum_fusion.16), channel_id=1, source_target_pairs={{0,2},{1,3},{4,6},{5,7},{8,10},{9,11},{12,14},{13,15},{16,18},{17,... | collective-permute-start | bytes 491528 | tf_op jit(solution)/shard_map/ppermute | solution.py:507
  164.6 22.9 %collective-permute-start.6 = (bf16[128,960]{0,1:T(8,128)(2,1)}, bf16[128,960]{0,1:T(8,128)(2,1)}, u32[]{:S(2)}, u32[]{:S(2)}) collective-permute-start(bf16[128,960]{0,1:T(8,128)(2,1)} %multiply_convert_fusion.4), channel_id=1, source_target_pairs={{0,2},{1,3},{2,0},{3,1},{4,6},{5,7},{6,4},{7,5},{8,10},{9,11},{10,... | collective-permute-start | bytes 737288 | tf_op jit(solution)/shard_map/ppermute | solution.py:290
  165.4 23.5 %collective-permute-start.5 = (bf16[128,960]{0,1:T(8,128)(2,1)}, bf16[128,960]{0,1:T(8,128)(2,1)}, u32[]{:S(2)}, u32[]{:S(2)}) collective-permute-start(bf16[128,960]{0,1:T(8,128)(2,1)} %multiply_convert_fusion.4), channel_id=1, source_target_pairs={{0,1},{1,0},{2,3},{3,2},{4,5},{5,4},{6,7},{7,6},{8,9},{9,8},{10,11... | collective-permute-start | bytes 737288 | tf_op jit(solution)/shard_map/ppermute | solution.py:290
  176.0 18.5 %collective-permute-start.14 = (bf16[128,960]{0,1:T(8,128)(2,1)}, bf16[128,960]{0,1:T(8,128)(2,1)S(1)}, u32[]{:S(2)}, u32[]{:S(2)}) collective-permute-start(bf16[128,960]{0,1:T(8,128)(2,1)} %bitcast_convert_fusion), channel_id=1, source_target_pairs={{0,1},{1,0},{2,3},{3,2},{4,5},{5,4},{6,7},{7,6},{8,9},{9,8},{10,11... | collective-permute-start | bytes 737288 | tf_op jit(solution)/shard_map/ppermute | solution.py:290
  187.5 146.4 %collective-permute-start.24 = (bf16[128,240]{0,1:T(8,128)(2,1)}, bf16[128,240]{0,1:T(8,128)(2,1)}, u32[]{:S(2)}, u32[]{:S(2)}) collective-permute-start(bf16[128,240]{0,1:T(8,128)(2,1)} %get-tuple-element.57), channel_id=1, source_target_pairs={{0,3},{1,2},{2,1},{3,0},{4,7},{5,6},{6,5},{7,4},{8,11},{9,10},{10,... | collective-permute-start | bytes 184328 | tf_op jit(solution)/shard_map/ppermute | solution.py:307
  188.9 145.1 %collective-permute-start.23 = (bf16[128,240]{0,1:T(8,128)(2,1)}, bf16[128,240]{0,1:T(8,128)(2,1)}, u32[]{:S(2)}, u32[]{:S(2)}) collective-permute-start(bf16[128,240]{0,1:T(8,128)(2,1)} %get-tuple-element.58), channel_id=1, source_target_pairs={{0,2},{1,3},{2,0},{3,1},{4,6},{5,7},{6,4},{7,5},{8,10},{9,11},{10,... | collective-permute-start | bytes 184328 | tf_op jit(solution)/shard_map/ppermute | solution.py:307
  220.1 60.8 %collective-permute-start.17 = (bf16[128,960]{0,1:T(8,128)(2,1)}, bf16[128,960]{0,1:T(8,128)(2,1)}, u32[]{:S(2)}, u32[]{:S(2)}) collective-permute-start(bf16[128,960]{0,1:T(8,128)(2,1)} %get-tuple-element.22), channel_id=1, source_target_pairs={{0,1},{1,0},{2,3},{3,2},{4,5},{5,4},{6,7},{7,6},{8,9},{9,8},{10,11... | collective-permute-start | bytes 737288 | tf_op jit(solution)/shard_map/ppermute | solution.py:297
  222.9 61.0 %collective-permute-start.19 = (bf16[128,960]{0,1:T(8,128)(2,1)}, bf16[128,960]{0,1:T(8,128)(2,1)}, u32[]{:S(2)}, u32[]{:S(2)}) collective-permute-start(bf16[128,960]{0,1:T(8,128)(2,1)} %get-tuple-element.23), channel_id=1, source_target_pairs={{0,3},{1,2},{2,1},{3,0},{4,7},{5,6},{6,5},{7,4},{8,11},{9,10},{10,... | collective-permute-start | bytes 737288 | tf_op jit(solution)/shard_map/ppermute | solution.py:297
  224.3 61.0 %collective-permute-start.18 = (bf16[128,960]{0,1:T(8,128)(2,1)}, bf16[128,960]{0,1:T(8,128)(2,1)}, u32[]{:S(2)}, u32[]{:S(2)}) collective-permute-start(bf16[128,960]{0,1:T(8,128)(2,1)} %get-tuple-element.24), channel_id=1, source_target_pairs={{0,2},{1,3},{2,0},{3,1},{4,6},{5,7},{6,4},{7,5},{8,10},{9,11},{10,... | collective-permute-start | bytes 737288 | tf_op jit(solution)/shard_map/ppermute | solution.py:297
  279.5 144.5 %reduce-scatter.7.cloned.1.call-start = ((), (), s32[]{:S(2)}) async-start(), calls=%async_computation.4 | async-start | bytes 1382400
  283.9 13.5 %collective-permute-start.13 = (bf16[128,960]{0,1:T(8,128)(2,1)S(1)}, bf16[128,960]{0,1:T(8,128)(2,1)S(1)}, u32[]{:S(2)}, u32[]{:S(2)}) collective-permute-start(bf16[128,960]{0,1:T(8,128)(2,1)S(1)} %get-tuple-element.26), channel_id=1, source_target_pairs={{0,3},{1,2},{2,1},{3,0},{4,7},{5,6},{6,5},{7,4},{8,11},{9,10},{10,... | collective-permute-start | bytes 737288 | tf_op jit(solution)/shard_map/ppermute | solution.py:297
  285.4 19.4 %collective-permute-start.12 = (bf16[128,960]{0,1:T(8,128)(2,1)S(1)}, bf16[128,960]{0,1:T(8,128)(2,1)S(1)}, u32[]{:S(2)}, u32[]{:S(2)}) collective-permute-start(bf16[128,960]{0,1:T(8,128)(2,1)S(1)} %get-tuple-element.27), channel_id=1, source_target_pairs={{0,2},{1,3},{2,0},{3,1},{4,6},{5,7},{6,4},{7,5},{8,10},{9,11},{10,... | collective-permute-start | bytes 737288 | tf_op jit(solution)/shard_map/ppermute | solution.py:297
  293.1 44.5 %collective-permute-start.22 = (bf16[128,240]{0,1:T(8,128)(2,1)}, bf16[128,240]{0,1:T(8,128)(2,1)S(1)}, u32[]{:S(2)}, u32[]{:S(2)}) collective-permute-start(bf16[128,240]{0,1:T(8,128)(2,1)} %get-tuple-element.59), channel_id=1, source_target_pairs={{0,1},{1,0},{2,3},{3,2},{4,5},{5,4},{6,7},{7,6},{8,9},{9,8},{10,11... | collective-permute-start | bytes 184328 | tf_op jit(solution)/shard_map/ppermute | solution.py:307
  312.6 21.3 %collective-permute-start.21 = (bf16[1,128,640]{1,2,0:T(8,128)(2,1)S(1)}, bf16[1,128,640]{1,2,0:T(8,128)(2,1)S(1)}, u32[]{:S(2)}, u32[]{:S(2)}) collective-permute-start(bf16[1,128,640]{1,2,0:T(8,128)(2,1)S(1)} %get-tuple-element.45), channel_id=1, source_target_pairs={{2,0},{3,1},{6,4},{7,5},{10,8},{11,9},{14,12},{15,13},{18,16},{19,... | collective-permute-start | bytes 491528 | tf_op jit(solution)/shard_map/ppermute | solution.py:582
  319.1 19.4 %collective-permute-start.33 = (bf16[128,240]{0,1:T(8,128)(2,1)}, bf16[128,240]{0,1:T(8,128)(2,1)S(1)}, u32[]{:S(2)}, u32[]{:S(2)}) collective-permute-start(bf16[128,240]{0,1:T(8,128)(2,1)} %get-tuple-element.61), channel_id=1, source_target_pairs={{0,3},{1,2},{2,1},{3,0},{4,7},{5,6},{6,5},{7,4},{8,11},{9,10},{10,... | collective-permute-start | bytes 184328 | tf_op jit(solution)/shard_map/ppermute | solution.py:307
  337.6 30.8 %collective-permute-start.35 = (bf16[128,960]{0,1:T(8,128)(2,1)S(1)}, bf16[128,960]{0,1:T(8,128)(2,1)S(1)}, u32[]{:S(2)}, u32[]{:S(2)}) collective-permute-start(bf16[128,960]{0,1:T(8,128)(2,1)S(1)} %get-tuple-element.10), channel_id=1, source_target_pairs={{0,2},{1,3},{2,0},{3,1},{4,6},{5,7},{6,4},{7,5},{8,10},{9,11},{10,... | collective-permute-start | bytes 737288 | tf_op jit(solution)/shard_map/ppermute | solution.py:290
  338.5 29.9 %collective-permute-start.34 = (bf16[128,960]{0,1:T(8,128)(2,1)S(1)}, bf16[128,960]{0,1:T(8,128)(2,1)S(1)}, u32[]{:S(2)}, u32[]{:S(2)}) collective-permute-start(bf16[128,960]{0,1:T(8,128)(2,1)S(1)} %get-tuple-element.10), channel_id=1, source_target_pairs={{0,1},{1,0},{2,3},{3,2},{4,5},{5,4},{6,7},{7,6},{8,9},{9,8},{10,11... | collective-permute-start | bytes 737288 | tf_op jit(solution)/shard_map/ppermute | solution.py:290
  346.6 21.8 %collective-permute-start.27 = (bf16[128,960]{0,1:T(8,128)(2,1)S(1)}, bf16[128,960]{0,1:T(8,128)(2,1)S(1)}, u32[]{:S(2)}, u32[]{:S(2)}) collective-permute-start(bf16[128,960]{0,1:T(8,128)(2,1)S(1)} %bitcast.301), channel_id=1, source_target_pairs={{0,3},{1,2},{2,1},{3,0},{4,7},{5,6},{6,5},{7,4},{8,11},{9,10},{10,... | collective-permute-start | bytes 737288 | tf_op jit(solution)/shard_map/ppermute | solution.py:290
  346.7 35.3 %collective-permute-start.26 = (bf16[128,960]{0,1:T(8,128)(2,1)S(1)}, bf16[128,960]{0,1:T(8,128)(2,1)}, u32[]{:S(2)}, u32[]{:S(2)}) collective-permute-start(bf16[128,960]{0,1:T(8,128)(2,1)S(1)} %bitcast.302), channel_id=1, source_target_pairs={{0,2},{1,3},{2,0},{3,1},{4,6},{5,7},{6,4},{7,5},{8,10},{9,11},{10,... | collective-permute-start | bytes 737288 | tf_op jit(solution)/shard_map/ppermute | solution.py:290
  346.8 35.3 %collective-permute-start.25 = (bf16[128,960]{0,1:T(8,128)(2,1)S(1)}, bf16[128,960]{0,1:T(8,128)(2,1)}, u32[]{:S(2)}, u32[]{:S(2)}) collective-permute-start(bf16[128,960]{0,1:T(8,128)(2,1)S(1)} %bitcast.303), channel_id=1, source_target_pairs={{0,1},{1,0},{2,3},{3,2},{4,5},{5,4},{6,7},{7,6},{8,9},{9,8},{10,11... | collective-permute-start | bytes 737288 | tf_op jit(solution)/shard_map/ppermute | solution.py:290
  368.4 16.1 %collective-permute-start.30 = (bf16[128,640]{0,1:T(8,128)(2,1)S(1)}, bf16[128,640]{0,1:T(8,128)(2,1)S(1)}, u32[]{:S(2)}, u32[]{:S(2)}) collective-permute-start(bf16[128,640]{0,1:T(8,128)(2,1)S(1)} %pad_maximum_fusion.17), channel_id=1, source_target_pairs={{0,3},{1,2},{2,1},{3,0},{4,7},{5,6},{6,5},{7,4},{8,11},{9,10},{10,... | collective-permute-start | bytes 491528 | tf_op jit(solution)/shard_map/ppermute | solution.py:290
  368.4 17.1 %collective-permute-start.29 = (bf16[128,640]{0,1:T(8,128)(2,1)S(1)}, bf16[128,640]{0,1:T(8,128)(2,1)S(1)}, u32[]{:S(2)}, u32[]{:S(2)}) collective-permute-start(bf16[128,640]{0,1:T(8,128)(2,1)S(1)} %pad_maximum_fusion.17), channel_id=1, source_target_pairs={{0,2},{1,3},{2,0},{3,1},{4,6},{5,7},{6,4},{7,5},{8,10},{9,11},{10,... | collective-permute-start | bytes 491528 | tf_op jit(solution)/shard_map/ppermute | solution.py:290
  368.4 17.0 %collective-permute-start.28 = (bf16[128,640]{0,1:T(8,128)(2,1)S(1)}, bf16[128,640]{0,1:T(8,128)(2,1)S(1)}, u32[]{:S(2)}, u32[]{:S(2)}) collective-permute-start(bf16[128,640]{0,1:T(8,128)(2,1)S(1)} %pad_maximum_fusion.17), channel_id=1, source_target_pairs={{0,1},{1,0},{2,3},{3,2},{4,5},{5,4},{6,7},{7,6},{8,9},{9,8},{10,11... | collective-permute-start | bytes 491528 | tf_op jit(solution)/shard_map/ppermute | solution.py:290
  409.0 16.7 %collective-permute-start.39 = (bf16[450,128]{1,0:T(8,128)(2,1)S(1)}, bf16[450,128]{1,0:T(8,128)(2,1)S(1)}, u32[]{:S(2)}, u32[]{:S(2)}) collective-permute-start(bf16[450,128]{1,0:T(8,128)(2,1)S(1)} %get-tuple-element.49), channel_id=1, source_target_pairs={{0,1},{1,0},{2,3},{3,2},{4,5},{5,4},{6,7},{7,6},{8,9},{9,8},{10,11... | collective-permute-start | bytes 345608 | tf_op jit(solution)/shard_map/ppermute | solution.py:307
  410.7 15.1 %collective-permute-start.38 = (bf16[450,128]{1,0:T(8,128)(2,1)S(1)}, bf16[450,128]{1,0:T(8,128)(2,1)S(1)}, u32[]{:S(2)}, u32[]{:S(2)}) collective-permute-start(bf16[450,128]{1,0:T(8,128)(2,1)S(1)} %get-tuple-element.50), channel_id=1, source_target_pairs={{0,2},{1,3},{2,0},{3,1},{4,6},{5,7},{6,4},{7,5},{8,10},{9,11},{10,... | collective-permute-start | bytes 345608 | tf_op jit(solution)/shard_map/ppermute | solution.py:307
  411.7 14.1 %collective-permute-start.37 = (bf16[450,128]{1,0:T(8,128)(2,1)S(1)}, bf16[450,128]{1,0:T(8,128)(2,1)S(1)}, u32[]{:S(2)}, u32[]{:S(2)}) collective-permute-start(bf16[450,128]{1,0:T(8,128)(2,1)S(1)} %get-tuple-element.51), channel_id=1, source_target_pairs={{0,3},{1,2},{2,1},{3,0},{4,7},{5,6},{6,5},{7,4},{8,11},{9,10},{10,... | collective-permute-start | bytes 345608 | tf_op jit(solution)/shard_map/ppermute | solution.py:307
  (71 other events, 634.9 us)
Sparse Core Ops, SparseCore 0:
  27.8 34.6 all-gather.4
  65.0 39.7 all-gather.2
  279.6 48.5 reduce-scatter.8
  390.0 33.9 reduce-scatter.6

commit v2 on v0

--- a/solution.py
+++ b/solution.py
@@ -1,6 +1,8 @@
 import jax
 import jax.numpy as jnp
 from jax import lax
+from jax.experimental import pallas as pl
+from jax.experimental.pallas import tpu as pltpu
 from jax.sharding import PartitionSpec as P
 
 D = 960
@@ -93,7 +95,7 @@
     )
 
 
-def body(hidden_in, segments, attn_flat, mlp_flat, norm_one, norm_two, cotangent):
+def body_rows(hidden_in, segments, attn_flat, mlp_flat, norm_one, norm_two, cotangent):
     seq_count, local_len, model_width = hidden_in.shape
     seq_len = segments.shape[1]
     row_count = seq_count * local_len
@@ -270,6 +272,863 @@
     )
 
 
+def gain_total(gain_rows):
+    total = gain_rows
+    for step in range(1, lax.axis_size("ctx")):
+        total = total + lax.ppermute(gain_rows, "ctx", swap_pairs("ctx", step))
+    step = 1
+    while step < lax.axis_size("dp"):
+        total = total + lax.ppermute(total, "dp", swap_pairs("dp", step))
+        step = 2 * step
+    return total
+
+
+def swap_pairs(axis, step):
+    return [(place, place ^ step) for place in range(lax.axis_size(axis))]
+
+
+def spread(rows):
+    return [rows] + [
+        lax.ppermute(rows, "ctx", swap_pairs("ctx", step)) for step in range(1, lax.axis_size("ctx"))
+    ]
+
+
+def returned(terms):
+    return [
+        lax.ppermute(term, "ctx", swap_pairs("ctx", step + 1)) for step, term in enumerate(terms)
+    ]
+
+
+def trade(blocks):
+    here = lax.axis_index("ctx")
+    got = [lax.dynamic_index_in_dim(blocks, here, 0, False)]
+    for step in range(1, lax.axis_size("ctx")):
+        block = lax.dynamic_index_in_dim(blocks, here ^ step, 0, False)
+        got.append(lax.ppermute(block, "ctx", swap_pairs("ctx", step)))
+    return got
+
+
+def in_order(pieces):
+    here = lax.axis_index("ctx")
+    step = 1
+    while step < len(pieces):
+        bit = (here & step) != 0
+        pieces = [
+            jnp.where(bit, pieces[place ^ step], pieces[place]) for place in range(len(pieces))
+        ]
+        step = 2 * step
+    return jnp.stack(pieces)
+
+
+def columns_apply(dp_count, ctx_count, rows):
+    unit = FFN // 128
+    return (
+        rows % unit == 0
+        and FFN % (128 * ctx_count) == 0
+        and D % ctx_count == 0
+        and ctx_count & (ctx_count - 1) == 0
+        and dp_count & (dp_count - 1) == 0
+        and rows % ctx_count == 0
+        and (2 * (D // ctx_count) % (rows // unit)) * unit % ctx_count == 0
+        and (rows - (2 * (D // ctx_count) % (rows // unit)) * unit) % (ctx_count * 2 * D // 128) == 0
+        and rows % (2 * D // 128) == 0
+    )
+
+
+def mlp_sizes(rows, ctx_count):
+    unit = FFN // 128
+    held = rows // unit
+    tall = 2 * (D // ctx_count)
+    return unit, unit // ctx_count, held, tall // held, tall % held
+
+
+def trade_mlp(flat):
+    ctx_count = lax.axis_size("ctx")
+    place = lax.axis_index("dp")
+    rows = flat.shape[0]
+    unit, part, held, edge, rest = mlp_sizes(rows, ctx_count)
+    cut = rest * unit
+
+    def by_column(block, count):
+        return (
+            block.reshape(count, ctx_count, part, 128)
+            .transpose(1, 0, 2, 3)
+            .reshape(ctx_count, count * part, 128)
+        )
+
+    full = by_column(flat, held)
+    tail = flat[cut:].reshape(ctx_count, -1, 128)
+    mixed = jnp.concatenate([by_column(flat[:cut], rest), tail], axis=1)
+    got = in_order(trade(jnp.where(place < edge, full, mixed)))
+    kept = jnp.concatenate([got[:, : rest * part], tail], axis=1)
+    block = jnp.where(
+        place < edge, got, jnp.where(place == edge, kept, flat.reshape(ctx_count, -1, 128))
+    )
+    return block.reshape(rows, 128)
+
+
+def scatter_mlp(terms):
+    ctx_count = lax.axis_size("ctx")
+    place = lax.axis_index("dp")
+    rows = terms.shape[0] // lax.axis_size("dp")
+    unit, part, held, edge, rest = mlp_sizes(rows, ctx_count)
+    own = lax.psum_scatter(terms, "dp", scatter_dimension=0, tiled=True)
+    blocks = own.reshape(ctx_count, rows // ctx_count, 128)
+    got = in_order(trade(blocks))
+
+    def by_row(block, count):
+        return block.reshape(ctx_count, count, part, 128).transpose(1, 0, 2, 3).reshape(-1, 128)
+
+    full = by_row(got, held)
+    mixed = jnp.concatenate(
+        [by_row(got[:, : rest * part], rest), blocks[:, rest * part :].reshape(-1, 128)], axis=0
+    )
+    out = jnp.where(place < edge, full, jnp.where(place == edge, mixed, own))
+    return out.astype(jnp.float32)
+
+
+VMEM_BYTES = 56 * 1024 * 1024
+LANES = 128
+HALF = LANES // 2
+
+
+def kernel_call(kernel, outs, scratch, *args):
+    return pl.pallas_call(
+        kernel,
+        out_shape=[jax.ShapeDtypeStruct(shape, dtype) for shape, dtype in outs],
+        scratch_shapes=[pltpu.VMEM(shape, dtype) for shape, dtype in scratch],
+        compiler_params=pltpu.CompilerParams(vmem_limit_bytes=VMEM_BYTES),
+    )(*args)
+
+
+def low_lanes(rows):
+    return lax.broadcasted_iota(jnp.int32, (rows, LANES), 1) < HALF
+
+
+def dot_nt(left, right):
+    return lax.dot_general(
+        left, right, (((1,), (1,)), ((), ())), preferred_element_type=jnp.float32
+    )
+
+
+def dot_nn(left, right):
+    return jnp.dot(left, right, preferred_element_type=jnp.float32)
+
+
+def pair_rows(flat_ref, base, pairs, width, offset, put):
+    halves = width // HALF
+    tiles = [flat_ref[pl.ds(base + step, pairs, stride=halves), :] for step in range(halves)]
+    rolled = {}
+    mask = low_lanes(pairs)
+
+    def roll(index):
+        index = min(max(index, 0), halves - 1)
+        if index not in rolled:
+            rolled[index] = pltpu.roll(tiles[index], HALF, 1)
+        return rolled[index]
+
+    for parity in range(2):
+        for tile in range((halves + offset + 1) // 2):
+            first = parity * halves - offset + 2 * tile
+            if first % 2 == 0:
+                put(tile, parity, tiles[first // 2])
+            else:
+                put(tile, parity, jnp.where(mask, roll(first // 2), roll(first // 2 + 1)))
+
+
+def flat_rows(get, flat_ref, base, pairs, width, offset):
+    halves = width // HALF
+    mask = low_lanes(pairs)
+    blocks, rolled = {}, {}
+
+    def half(index, want):
+        parity, index = divmod(index, halves)
+        tile, side = divmod(index + offset, 2)
+        key = (tile, parity)
+        if key not in blocks:
+            blocks[key] = get(tile, parity)
+        if side == want:
+            return blocks[key]
+        if key not in rolled:
+            rolled[key] = pltpu.roll(blocks[key], HALF, 1)
+        return rolled[key]
+
+    for step in range(halves):
+        left, right = half(2 * step, 0), half(2 * step + 1, 1)
+        flat_ref[pl.ds(base + step, pairs, stride=halves), :] = (
+            left if left is right else jnp.where(mask, left, right)
+        )
+
+
+def partner_lanes(block):
+    quarter = HEAD_DIM // 2
+    lane = lax.broadcasted_iota(jnp.int32, block.shape, 1)
+    return jnp.where(
+        (lane & quarter) == 0,
+        pltpu.roll(block, LANES - quarter, 1),
+        pltpu.roll(block, quarter, 1),
+    )
+
+
+def attn_pieces(rows, dp_count, ctx_count):
+    runs = []
+    begin = 0
+    for height, width in (
+        (D, HEADS * HEAD_DIM),
+        (D, KV_HEADS * HEAD_DIM),
+        (D, KV_HEADS * HEAD_DIM),
+        (HEADS * HEAD_DIM, D),
+    ):
+        block = height // ctx_count
+        span = block * width // LANES
+        matrix = []
+        for ctx in range(ctx_count):
+            at = begin
+            while at < begin + span:
+                part, inside = divmod(at, rows)
+                size = min(rows - inside, begin + span - at)
+                matrix.append(
+                    (
+                        ctx * block + (at - begin) * LANES // width,
+                        size * LANES // width,
+                        (part * ctx_count + ctx) * rows + inside,
+                        size,
+                    )
+                )
+                at = at + size
+        runs.append(matrix)
+        begin = begin + span
+    return runs
+
+
+def attn_fits(rows, dp_count, ctx_count):
+    widths = (HEADS * HEAD_DIM, KV_HEADS * HEAD_DIM, KV_HEADS * HEAD_DIM, D)
+    return D % ctx_count == 0 and all(
+        (2 * width) % LANES == 0
+        and (width // HALF) % 2 == 1
+        and size % (2 * width // LANES) == 0
+        and row % 2 == 0
+        for width, matrix in zip(widths, attn_pieces(rows, dp_count, ctx_count))
+        for row, _, _, size in matrix
+    )
+
+
+def project(flat, residual, gain, cosine, sine, rows, dp_count, ctx_count):
+    tokens = residual.shape[0]
+    qwidth, kwidth = HEADS * HEAD_DIM, KV_HEADS * HEAD_DIM
+    whole = qwidth + 2 * kwidth
+    runs = attn_pieces(rows, dp_count, ctx_count)
+    total = flat.shape[0]
+    qtiles = -(-qwidth // LANES)
+    ktile, koff = divmod(qwidth // HALF, 2)
+    vtile, voff = divmod((qwidth + kwidth) // HALF, 2)
+    ktiles = (kwidth // HALF + koff + 1) // 2
+    vtiles = (kwidth // HALF + voff + 1) // 2
+
+    def kernel(
+        flat_ref, res_ref, gain_ref, cos_ref, sin_ref,
+        normed_ref, query_ref, kv_ref, wide_ref, out_ref, long_ref, tile_ref,
+    ):
+        long_ref[...] = flat_ref[...].astype(jnp.float32)
+        places = ((0, 0, 0), (qtiles, koff, ktile), (qtiles + ktiles, voff, vtile))
+        for (slot, offset, _), matrix, width in zip(places, runs, (qwidth, kwidth, kwidth)):
+            for row, count, base, size in matrix:
+                def put(tile, parity, block, slot=slot, row=row, count=count):
+                    tile_ref[slot + tile, pl.ds(row + parity, count // 2, stride=2), :] = block
+
+                pair_rows(long_ref, base, count // 2, width, offset, put)
+        mask = low_lanes(D)
+        for tile in range(-(-whole // LANES)):
+            held = [
+                tile_ref[slot + tile - first]
+                for (slot, _, first), count in zip(places, (qtiles, ktiles, vtiles))
+                if first <= tile < first + count
+            ]
+            block = held[0] if len(held) == 1 else jnp.where(mask, held[0], held[1])
+            width = min(LANES, whole - tile * LANES)
+            wide_ref[:, tile * LANES : tile * LANES + width] = block[:, :width].astype(jnp.bfloat16)
+        residual = res_ref[...]
+        inverse = lax.rsqrt(jnp.mean(residual * residual, axis=-1, keepdims=True) + EPS)
+        normed = (residual * inverse * gain_ref[...]).astype(jnp.bfloat16)
+        normed_ref[...] = normed
+        product = dot_nn(normed, wide_ref[...])
+        turned = []
+        for tile in range((qwidth + kwidth) // LANES):
+            block = product[:, tile * LANES : (tile + 1) * LANES]
+            turned.append(
+                (block * cos_ref[...] + partner_lanes(block) * sin_ref[...]).astype(jnp.bfloat16)
+            )
+        turned = jnp.concatenate(turned, axis=1)
+        query_ref[...] = turned[:, :qwidth]
+        kv_ref[:, :kwidth] = turned[:, qwidth:]
+        kv_ref[:, kwidth:] = product[:, qwidth + kwidth :].astype(jnp.bfloat16)
+        for row, count, base, size in runs[3]:
+            def put(tile, parity, block, row=row, count=count):
+                tile_ref[tile, pl.ds(row + parity, count // 2, stride=2), :] = block
+
+            pair_rows(long_ref, base, count // 2, D, 0, put)
+        for tile in range(-(-D // LANES)):
+            width = min(LANES, D - tile * LANES)
+            out_ref[:, tile * LANES : tile * LANES + width] = tile_ref[tile][:, :width].astype(
+                jnp.bfloat16
+            )
+
+    low = jnp.bfloat16
+    return kernel_call(
+        kernel,
+        [
+            ((tokens, D), low),
+            ((tokens, qwidth), low),
+            ((tokens, 2 * kwidth), low),
+            ((D, whole), low),
+            ((qwidth, D), low),
+        ],
+        [((total, LANES), jnp.float32), ((qtiles + ktiles + vtiles, D, LANES), jnp.float32)],
+        flat, residual, gain, cosine, sine,
+    )
+
+
+def group_rows(ref, group, groups):
+    first = group * groups * HEAD_DIM
+    return jnp.concatenate(
+        [ref[:, first + g * HEAD_DIM : first + (g + 1) * HEAD_DIM] for g in range(groups)], axis=0
+    )
+
+
+def group_allowed(seg_ref, near_ref, tokens, near_len, groups):
+    query = lax.broadcasted_iota(jnp.int32, (tokens, near_len), 0)
+    key = lax.broadcasted_iota(jnp.int32, (tokens, near_len), 1) - (near_len - tokens)
+    allowed = (seg_ref[...] == near_ref[...]) & (key <= query)
+    return allowed
+
+
+def attend(query, kv_parts, seg_col, seg_near, residual, w_out, gain):
+    tokens = query.shape[0]
+    parts = len(kv_parts)
+    near_len = parts * tokens
+    groups = HEADS // KV_HEADS
+    kwidth = KV_HEADS * HEAD_DIM
+    scale = HEAD_DIM ** (-0.5)
+
+    def kernel(*refs):
+        query_ref = refs[0]
+        kv_refs = refs[1 : 1 + parts]
+        seg_ref, near_ref, res_ref, out_ref, gain_ref = refs[1 + parts : 6 + parts]
+        near_kv_ref, mix_ref, log_ref, mid_ref, normed_ref = refs[6 + parts :]
+        for part in range(parts):
+            near_kv_ref[part * tokens : (part + 1) * tokens, :] = kv_refs[part][...]
+        allowed = group_allowed(seg_ref, near_ref, tokens, near_len, groups)
+        allowed = jnp.concatenate([allowed.astype(jnp.float32)] * groups, axis=0) > 0.5
+        mixes, logs = [], []
+        for group in range(KV_HEADS):
+            at = group * HEAD_DIM
+            key = near_kv_ref[:, at : at + HEAD_DIM]
+            value = near_kv_ref[:, kwidth + at : kwidth + at + HEAD_DIM]
+            scores = dot_nt(group_rows(query_ref, group, groups), key) * scale
+            scores = jnp.where(allowed, scores, -jnp.inf)
+            top = jnp.max(scores, axis=-1, keepdims=True)
+            total = top + jnp.log(jnp.sum(jnp.exp(scores - top), axis=-1, keepdims=True))
+            probs = jnp.exp(scores - total).astype(jnp.bfloat16)
+            mix = dot_nn(probs, value).astype(jnp.bfloat16)
+            for g in range(groups):
+                mixes.append(mix[g * tokens : (g + 1) * tokens])
+                logs.append(total[g * tokens : (g + 1) * tokens])
+        for head in range(HEADS):
+            log_ref[:, head : head + 1] = logs[head]
+        head_mix = jnp.concatenate(mixes, axis=1)
+        mix_ref[...] = head_mix
+        middle = res_ref[...] + dot_nn(head_mix, out_ref[...])
+        mid_ref[...] = middle
+        inverse = lax.rsqrt(jnp.mean(middle * middle, axis=-1, keepdims=True) + EPS)
+        normed_ref[...] = (middle * inverse * gain_ref[...]).astype(jnp.bfloat16)
+
+    low, wide = jnp.bfloat16, jnp.float32
+    return kernel_call(
+        kernel,
+        [
+            ((near_len, 2 * kwidth), low),
+            ((tokens, HEADS * HEAD_DIM), low),
+            ((tokens, LANES), wide),
+            ((tokens, D), wide),
+            ((tokens, D), low),
+        ],
+        [],
+        query, *kv_parts, seg_col, seg_near, residual, w_out, gain,
+    )
+
+
+def mlp_pieces(rows, dp_count, ctx_count):
+    unit, part, held, edge, rest = mlp_sizes(rows, ctx_count)
+    share = rows // ctx_count
+    block = D // ctx_count
+    gate, up, down = [], [], []
+    for ctx in range(ctx_count):
+        for dp in range(edge + (rest > 0)):
+            count = held if dp < edge else rest
+            row, stop = dp * held, dp * held + count
+            base = (dp * ctx_count + ctx) * share
+            for matrix, begin, end in ((gate, 0, block), (up, block, 2 * block)):
+                low, high = max(row, begin), min(stop, end)
+                if low < high:
+                    matrix.append((ctx * block + low - begin, high - low, base + (low - row) * part))
+    cut = rest * part
+    at = 0
+    for ctx in range(ctx_count):
+        size = share - cut
+        down.append((at * LANES // D, size * LANES // D, (edge * ctx_count + ctx) * share + cut))
+        at = at + size
+    for dp in range(edge + 1, dp_count):
+        down.append((at * LANES // D, rows * LANES // D, dp * rows))
+        at = at + rows
+    return part, gate, up, down
+
+
+def unpack_mlp(flat, cot_slots, rows, dp_count, ctx_count):
+    part, gate, up, down = mlp_pieces(rows, dp_count, ctx_count)
+    hidden = part * LANES
+    tiles = -(-D // LANES)
+    tokens = cot_slots[0].shape[0]
+    count = len(cot_slots)
+
+    def kernel(flat_ref, *refs):
+        cot_refs = refs[:count]
+        gate_ref, up_ref, down_ref, act_ref, long_ref, tile_ref, turn_ref = refs[count:]
+        long_ref[...] = flat_ref[...].astype(jnp.float32)
+        for row, size, base in down:
+            def put(tile, parity, block, row=row, size=size):
+                tile_ref[tile, pl.ds(row + parity, size // 2, stride=2), :] = block
+
+            pair_rows(long_ref, base, size // 2, D, 0, put)
+        for tile in range(tiles):
+            width = min(LANES, D - tile * LANES)
+            down_ref[:, tile * LANES : tile * LANES + width] = tile_ref[tile][:, :width].astype(
+                jnp.bfloat16
+            )
+        for slot in range(count):
+            act_ref[slot * tokens : (slot + 1) * tokens, :] = dot_nt(
+                cot_refs[slot][...], down_ref[...]
+            )
+        for runs, ref in ((gate, gate_ref), (up, up_ref)):
+            for row, size, base in runs:
+                for step in range(part):
+                    turn_ref[step, row : row + size, :] = long_ref[
+                        pl.ds(base + step, size, stride=part), :
+                    ]
+            for step in range(part):
+                ref[:, step * LANES : (step + 1) * LANES] = turn_ref[step].astype(jnp.bfloat16)
+
+    low, wide = jnp.bfloat16, jnp.float32
+    return kernel_call(
+        kernel,
+        [
+            ((D, hidden), low),
+            ((D, hidden), low),
+            ((hidden, D), low),
+            ((count * tokens, hidden), wide),
+        ],
+        [
+            (flat.shape, wide),
+            ((tiles, hidden, LANES), wide),
+            ((part, D, LANES), wide),
+        ],
+        flat, *cot_slots,
+    )
+
+
+def feed_forward(two_slots, w_gate, w_up, grad_active):
+    count = len(two_slots)
+    tokens = two_slots[0].shape[0]
+    hidden = w_gate.shape[1]
+
+    def kernel(*refs):
+        two_refs = refs[:count]
+        gate_ref, up_ref, act_ref = refs[count : count + 3]
+        active_ref, dgate_ref, dup_ref, own_ref = refs[count + 3 : count + 7]
+        term_refs = refs[count + 7 :]
+        for slot in list(range(1, count)) + [0]:
+            rows = slice(slot * tokens, (slot + 1) * tokens)
+            two = two_refs[slot][...]
+            gate = dot_nn(two, gate_ref[...])
+            up = dot_nn(two, up_ref[...])
+            grad = act_ref[rows, :]
+            sigmoid = jax.nn.sigmoid(gate)
+            active_ref[rows, :] = (gate * sigmoid * up).astype(jnp.bfloat16)
+            dgate = (grad * up * sigmoid * (1.0 + gate * (1.0 - sigmoid))).astype(jnp.bfloat16)
+            dup = (grad * gate * sigmoid).astype(jnp.bfloat16)
+            dgate_ref[rows, :] = dgate
+            dup_ref[rows, :] = dup
+            term = dot_nt(dgate, gate_ref[...]) + dot_nt(dup, up_ref[...])
+            if slot:
+                term_refs[slot - 1][...] = term.astype(jnp.bfloat16)
+            else:
+                own_ref[...] = term
+
+    low, wide = jnp.bfloat16, jnp.float32
+    return kernel_call(
+        kernel,
+        [((count * tokens, hidden), low)] * 3
+        + [((tokens, D), wide)]
+        + [((tokens, D), low)] * (count - 1),
+        [],
+        *two_slots, w_gate, w_up, grad_active,
+    )
+
+
+def mlp_grads(active, dgate, dup, two_slots, cot_slots, w_down, rows, dp_count, ctx_count):
+    count = len(two_slots)
+    tokens = two_slots[0].shape[0]
+    part, gate_runs, up_runs, down_runs = mlp_pieces(rows, dp_count, ctx_count)
+    tiles = -(-D // LANES)
+    hidden = part * LANES
+
+    def kernel(*refs):
+        active_ref, dgate_ref, dup_ref = refs[:3]
+        two_refs = refs[3 : 3 + count]
+        cot_refs = refs[3 + count : 3 + 2 * count]
+        down_ref = refs[3 + 2 * count]
+        flat_ref, own_ref = refs[4 + 2 * count : 6 + 2 * count]
+        term_refs = refs[6 + 2 * count : 5 + 3 * count]
+        long_ref, tile_ref, turn_ref = refs[5 + 3 * count :]
+        for slot in range(count):
+            term = dot_nn(active_ref[slot * tokens : (slot + 1) * tokens, :], down_ref[...])
+            if slot:
+                term_refs[slot - 1][...] = term.astype(jnp.bfloat16)
+            else:
+                own_ref[...] = term
+        two = jnp.concatenate([ref[...] for ref in two_refs], axis=0)
+        for runs, grad_ref in ((gate_runs, dgate_ref), (up_runs, dup_ref)):
+            value = left_dot(two, grad_ref[...])
+            for step in range(part):
+                turn_ref[step] = value[:, step * LANES : (step + 1) * LANES]
+            for row, size, base in runs:
+                for step in range(part):
+                    long_ref[pl.ds(base + step, size, stride=part), :] = turn_ref[
+                        step, row : row + size, :
+                    ]
+        cot = jnp.concatenate([ref[...] for ref in cot_refs], axis=0)
+        value = left_dot(active_ref[...], cot)
+        for tile in range(tiles):
+            width = min(LANES, D - tile * LANES)
+            tile_ref[tile, :, :width] = value[:, tile * LANES : tile * LANES + width]
+        for row, size, base in down_runs:
+            def get(tile, parity, row=row, size=size):
+                return tile_ref[tile, pl.ds(row + parity, size // 2, stride=2), :]
+
+            flat_rows(get, long_ref, base, size // 2, D, 0)
+        flat_ref[...] = long_ref[...].astype(jnp.bfloat16)
+
+    low, wide = jnp.bfloat16, jnp.float32
+    total = rows * dp_count
+    return kernel_call(
+        kernel,
+        [((total, LANES), low), ((tokens, D), wide)] + [((tokens, D), low)] * (count - 1),
+        [((total, LANES), wide), ((tiles, hidden, LANES), wide), ((part, D, LANES), wide)],
+        active, dgate, dup, *two_slots, *cot_slots, w_down,
+    )
+
+
+def middle_backward(own, others, middle, gain, cot_rows, w_out):
+    tokens = own.shape[0]
+    count = len(others)
+
+    def kernel(own_ref, *refs):
+        other_refs = refs[:count]
+        mid_ref, gain_ref, cot_ref, out_ref = refs[count : count + 4]
+        grad_ref, low_ref, mix_ref, sum_ref = refs[count + 4 :]
+        grad = own_ref[...]
+        for ref in other_refs:
+            grad = grad + ref[...].astype(jnp.float32)
+        middle = mid_ref[...]
+        inverse = lax.rsqrt(jnp.mean(middle * middle, axis=-1, keepdims=True) + EPS)
+        scaled = grad * gain_ref[...]
+        cubed = inverse * inverse * inverse
+        result = cot_ref[...] + (
+            inverse * scaled - middle * cubed * jnp.mean(scaled * middle, axis=-1, keepdims=True)
+        )
+        grad_ref[...] = result
+        low_ref[...] = result.astype(jnp.bfloat16)
+        mix_ref[...] = dot_nt(low_ref[...], out_ref[...]).astype(jnp.bfloat16)
+        sum_ref[...] = jnp.sum(grad * middle * inverse, axis=0, keepdims=True)
+
+    low, wide = jnp.bfloat16, jnp.float32
+    return kernel_call(
+        kernel,
+        [
+            ((tokens, D), wide),
+            ((tokens, D), low),
+            ((tokens, HEADS * HEAD_DIM), low),
+            ((1, D), wide),
+        ],
+        [],
+        own, *others, middle, gain, cot_rows, w_out,
+    )
+
+
+def attend_backward(query, near_kv, grad_mix, logs, seg_col, seg_near, cosine, sine):
+    tokens = query.shape[0]
+    near_len = near_kv.shape[0]
+    parts = near_len // tokens
+    groups = HEADS // KV_HEADS
+    qwidth, kwidth = HEADS * HEAD_DIM, KV_HEADS * HEAD_DIM
+    scale = HEAD_DIM ** (-0.5)
+    tiles = -(-qwidth // LANES)
+
+    def kernel(
+        query_ref, kv_ref, mix_ref, log_ref, seg_ref, near_ref, cos_ref, sin_ref, dquery_ref, own_ref,
+        *rest,
+    ):
+        part_refs = rest[: parts - 1]
+        turn_ref, term_ref = rest[parts - 1 :]
+        allowed = group_allowed(seg_ref, near_ref, tokens, near_len, groups)
+        allowed = jnp.concatenate([allowed.astype(jnp.float32)] * groups, axis=0) > 0.5
+        if tiles * LANES > qwidth:
+            turn_ref[:, qwidth:] = jnp.zeros((tokens, tiles * LANES - qwidth), jnp.float32)
+        for group in range(KV_HEADS):
+            at = group * HEAD_DIM
+            key = kv_ref[:, at : at + HEAD_DIM]
+            value = kv_ref[:, kwidth + at : kwidth + at + HEAD_DIM]
+            queries = group_rows(query_ref, group, groups)
+            mixes = group_rows(mix_ref, group, groups)
+            total = jnp.concatenate(
+                [log_ref[:, group * groups + g : group * groups + g + 1] for g in range(groups)],
+                axis=0,
+            )
+            scores = dot_nt(queries, key) * scale
+            probs = jnp.exp(jnp.where(allowed, scores, -jnp.inf) - total)
+            grad_probs = dot_nt(mixes, value)
+            grad_scores = probs * (grad_probs - jnp.sum(probs * grad_probs, axis=-1, keepdims=True))
+            grad_scores = (grad_scores * scale).astype(jnp.bfloat16)
+            dquery = dot_nn(grad_scores, key)
+            for g in range(groups):
+                first = (group * groups + g) * HEAD_DIM
+                turn_ref[:, first : first + HEAD_DIM] = dquery[g * tokens : (g + 1) * tokens]
+            term_ref[:, at : at + HEAD_DIM] = left_dot(grad_scores, queries)
+            term_ref[:, kwidth + at : kwidth + at + HEAD_DIM] = left_dot(
+                probs.astype(jnp.bfloat16), mixes
+            )
+        for part in range(parts - 1):
+            part_refs[part][...] = term_ref[part * tokens : (part + 1) * tokens, :].astype(
+                jnp.bfloat16
+            )
+        own_ref[...] = term_ref[near_len - tokens :, :]
+        for tile in range(tiles):
+            width = min(LANES, qwidth - tile * LANES)
+            block = turn_ref[:, tile * LANES : (tile + 1) * LANES]
+            block = block * cos_ref[...] - partner_lanes(block) * sin_ref[...]
+            dquery_ref[:, tile * LANES : tile * LANES + width] = block[:, :width].astype(
+                jnp.bfloat16
+            )
+
+    low, wide = jnp.bfloat16, jnp.float32
+    return kernel_call(
+        kernel,
+        [((tokens, qwidth), low), ((tokens, 2 * kwidth), wide)]
+        + [((tokens, 2 * kwidth), low)] * (parts - 1),
+        [((tokens, tiles * LANES), wide), ((near_len, 2 * kwidth), wide)],
+        query, near_kv, grad_mix, logs, seg_col, seg_near, cosine, sine,
+    )
+
+
+def own_kv(own, others, cosine, sine):
+    tokens = own.shape[0]
+    kwidth = KV_HEADS * HEAD_DIM
+
+    def kernel(own_ref, *refs):
+        other_refs, (cos_ref, sin_ref, out_ref) = refs[:-3], refs[-3:]
+        total = own_ref[...]
+        for ref in other_refs:
+            total = total + ref[...].astype(jnp.float32)
+        for tile in range(2 * kwidth // LANES):
+            block = total[:, tile * LANES : (tile + 1) * LANES]
+            if tile * LANES < kwidth:
+                turned = block * cos_ref[...] - partner_lanes(block) * sin_ref[...]
+                lane = lax.broadcasted_iota(jnp.int32, block.shape, 1)
+                block = jnp.where(lane < kwidth - tile * LANES, turned, block)
+            out_ref[:, tile * LANES : (tile + 1) * LANES] = block.astype(jnp.bfloat16)
+
+    return kernel_call(
+        kernel, [((tokens, 2 * kwidth), jnp.bfloat16)], [], own, *others, cosine, sine
+    )[0]
+
+
+def input_backward(grad_query, grad_kv, w_qkv, residual, gain, grad_middle):
+    tokens = residual.shape[0]
+    qwidth = HEADS * HEAD_DIM
+    whole = w_qkv.shape[1]
+
+    def kernel(query_ref, kv_ref, w_ref, res_ref, gain_ref, mid_ref, grad_ref, sum_ref, row_ref):
+        row_ref[:, :qwidth] = query_ref[...]
+        row_ref[:, qwidth:] = kv_ref[...]
+        grad = dot_nt(row_ref[...], w_ref[...])
+        residual = res_ref[...]
+        inverse = lax.rsqrt(jnp.mean(residual * residual, axis=-1, keepdims=True) + EPS)
+        scaled = grad * gain_ref[...]
+        cubed = inverse * inverse * inverse
+        grad_ref[...] = mid_ref[...] + (
+            inverse * scaled
+            - residual * cubed * jnp.mean(scaled * residual, axis=-1, keepdims=True)
+        )
+        sum_ref[...] = jnp.sum(grad * residual * inverse, axis=0, keepdims=True)
+
+    return kernel_call(
+        kernel,
+        [((tokens, D), jnp.float32), ((1, D), jnp.float32)],
+        [((tokens, whole), jnp.bfloat16)],
+        grad_query, grad_kv, w_qkv, residual, gain, grad_middle,
+    )
+
+
+def attn_grads(one_slots, mix_slots, query_slots, kv_slots, mid_slots, rows, dp_count):
+    count = len(one_slots)
+    block = one_slots[0].shape[1]
+    qwidth, kwidth = HEADS * HEAD_DIM, KV_HEADS * HEAD_DIM
+    tiles = -(-max(qwidth, D) // LANES)
+    total = rows * dp_count
+
+    def kernel(*refs):
+        ones, mixes, queries, kvs, mids = [
+            jnp.concatenate([ref[...] for ref in refs[k * count : (k + 1) * count]], axis=0)
+            for k in range(5)
+        ]
+        flat_ref, long_ref, tile_ref = refs[5 * count :]
+        base = 0
+        for left, right, parts in (
+            (ones, queries, ((0, qwidth),)),
+            (ones, kvs, ((0, kwidth), (kwidth, kwidth))),
+            (mixes, mids, ((0, D),)),
+        ):
+            value = left_dot(left, right)
+            span = value.shape[1]
+            for tile in range(-(-span // LANES)):
+                width = min(LANES, span - tile * LANES)
+                tile_ref[tile, :, :width] = value[:, tile * LANES : tile * LANES + width]
+            for first, width in parts:
+                lead, offset = divmod(first // HALF, 2)
+
+                def get(tile, parity, lead=lead):
+                    return tile_ref[lead + tile, pl.ds(parity, block // 2, stride=2), :]
+
+                flat_rows(get, long_ref, base, block // 2, width, offset)
+                base = base + block * width // LANES
+        flat_ref[...] = long_ref[...].astype(jnp.bfloat16)
+
+    return kernel_call(
+        kernel,
+        [((total, LANES), jnp.bfloat16)],
+        [((total, LANES), jnp.float32), ((tiles, block, LANES), jnp.float32)],
+        *one_slots, *mix_slots, *query_slots, *kv_slots, *mid_slots,
+    )[0]
+
+
+def body(hidden_in, segments, attn_flat, mlp_flat, norm_one, norm_two, cotangent):
+    dp_count, ctx_count = lax.axis_size("dp"), lax.axis_size("ctx")
+    if not (
+        hidden_in.shape[0] == 1
+        and columns_apply(dp_count, ctx_count, mlp_flat.shape[0])
+        and attn_fits(attn_flat.shape[0], dp_count, ctx_count)
+    ):
+        return body_rows(hidden_in, segments, attn_flat, mlp_flat, norm_one, norm_two, cotangent)
+    return body_columns(hidden_in, segments, attn_flat, mlp_flat, norm_one, norm_two, cotangent)
+
+
+def body_columns(hidden_in, segments, attn_flat, mlp_flat, norm_one, norm_two, cotangent):
+    tokens = hidden_in.shape[1]
+    seq_len = segments.shape[1]
+    low = jnp.bfloat16
+    dp_count = lax.axis_size("dp")
+    ctx_count = lax.axis_size("ctx")
+    attn_rows, mlp_rows = attn_flat.shape[0], mlp_flat.shape[0]
+    back = -(-(seq_len // 2 - 1) // tokens)
+    start_row = lax.axis_index("ctx") * tokens
+
+    attn_near = in_order(spread(attn_flat)).reshape(-1, 128)
+    mlp_near = trade_mlp(mlp_flat)
+    attn_whole = lax.all_gather(attn_near, "dp", axis=0, tiled=True)
+    mlp_near, attn_whole = lax.optimization_barrier((mlp_near, attn_whole))
+    mlp_whole = lax.all_gather(mlp_near, "dp", axis=0, tiled=True)
+
+    pos_local = lax.dynamic_slice_in_dim(positions_of(segments), start_row, tokens, 1)
+    seg_col = lax.dynamic_slice_in_dim(segments, start_row, tokens, 1).reshape(tokens, 1)
+    seg_near = lax.dynamic_slice_in_dim(
+        jnp.pad(segments, ((0, 0), (back * tokens, 0)), constant_values=-1),
+        start_row,
+        (back + 1) * tokens,
+        1,
+    )
+    cosine, sine = [table[:, 0] for table in rope_tables(pos_local.reshape(-1))]
+    heads = 128 // HEAD_DIM
+    cosine = jnp.concatenate([cosine, cosine] * heads, axis=1)
+    sine = jnp.concatenate([-sine, sine] * heads, axis=1)
+    gain_one, gain_two = norm_one.reshape(1, D), norm_two.reshape(1, D)
+
+    residual = hidden_in.reshape(tokens, D)
+    cot_rows = cotangent.reshape(tokens, D)
+    cot_slots = spread(cot_rows.astype(low))
+
+    def cols(rows):
+        return trade(rows.reshape(tokens, ctx_count, -1).transpose(1, 0, 2))
+
+    normed_one, query, kv_local, w_qkv, w_out = project(
+        attn_whole, residual, gain_one, cosine, sine, attn_rows, dp_count, ctx_count
+    )
+    one_slots = cols(normed_one)
+    up_pairs = [
+        [(place, place + step) for place in range(ctx_count - step)] for step in range(back + 1)
+    ]
+    down_pairs = [[(right, left) for left, right in pairs] for pairs in up_pairs]
+    kv_parts = [
+        lax.ppermute(kv_local, "ctx", up_pairs[step]) for step in range(back, 0, -1)
+    ] + [kv_local]
+    near_kv, head_mix, logs, middle, normed_two = attend(
+        query, kv_parts, seg_col, seg_near, residual, w_out, gain_two
+    )
+    two_slots = spread(normed_two)
+    mix_slots = cols(head_mix)
+
+    w_gate, w_up, w_down, grad_active = unpack_mlp(
+        mlp_whole, cot_slots, mlp_rows, dp_count, ctx_count
+    )
+    active, grad_gate, grad_up, *two_terms = feed_forward(two_slots, w_gate, w_up, grad_active)
+    two_others = returned(two_terms[1:])
+    mlp_terms, block_own, *block_terms = mlp_grads(
+        active, grad_gate, grad_up, two_slots, cot_slots, w_down, mlp_rows, dp_count, ctx_count
+    )
+    block_rows = middle + block_own
+    for moved in returned(block_terms):
+        block_rows = block_rows + moved.astype(jnp.float32)
+    mlp_grad = scatter_mlp(mlp_terms)
+
+    grad_middle, grad_mid_low, grad_mix, grad_gain_two = middle_backward(
+        two_terms[0], two_others, middle, gain_two, cot_rows, w_out
+    )
+    mid_slots = spread(grad_mid_low)
+    grad_query, kv_own, *kv_terms = attend_backward(
+        query, near_kv, grad_mix, logs, seg_col, seg_near, cosine, sine
+    )
+    kv_others = [
+        lax.ppermute(kv_terms[back - step], "ctx", down_pairs[step]) for step in range(1, back + 1)
+    ]
+    grad_kv = own_kv(kv_own, kv_others, cosine, sine)
+    query_slots = spread(grad_query)
+    kv_slots = spread(grad_kv)
+    attn_terms = attn_grads(
+        one_slots, mix_slots, query_slots, kv_slots, mid_slots, attn_rows, dp_count
+    )
+    attn_grad = lax.psum_scatter(attn_terms, "dp", scatter_dimension=0, tiled=True)
+    grad_in, grad_gain_one = input_backward(
+        grad_query, grad_kv, w_qkv, residual, gain_one, grad_middle
+    )
+    gain_sums = gain_total(jnp.concatenate([grad_gain_one, grad_gain_two], axis=0))
+    return (
+        block_rows.reshape(hidden_in.shape),
+        grad_in.reshape(hidden_in.shape),
+        attn_grad.astype(jnp.float32),
+        mlp_grad,
+        gain_sums[0],
+        gain_sums[1],
+    )
+
+
 def solution(mesh):
     in_specs = (
         P("dp", "ctx", None),

time: 646 us -> 341 us (0.53); the launches traced: 637 us -> 340 us
  blocking collectives: 232 us -> 0 us
  local copies, waits for them, and re-layouts: 147 us -> 17.5 us
  Pallas kernels: 0 us -> 59.1 us
  starting transfers between devices: 37.2 us -> 93.8 us
  matrix products: 53.6 us -> 0 us
  waiting for transfers between devices: 126 us -> 144 us
  other arithmetic: 26 us -> 10.5 us
    all_gather x6 -> x0, blocking collectives: 193 us -> none  [the longest x1 58.9 us: body(): lax.all_gather(grad_query, 'ctx', axis=0, tiled=True)]
    ppermute x0 -> x46, waiting for transfers between devices: none -> 120 us  [the longest x18 42.1 us: spread(): lax.ppermute(rows, 'ctx', swap_pairs('ctx', step))]
    ppermute x0 -> x46, starting transfers between devices: none -> 93.6 us  [the longest x18 42.6 us: spread(): lax.ppermute(rows, 'ctx', swap_pairs('ctx', step))]
    all_gather x4 -> x2, waiting for transfers between devices: 105 us -> 24.3 us  [the longest x1 24.3 us: body_columns(): attn_whole = lax.all_gather(attn_near, 'dp', axis=0, tiled=True)]
    reshape x13 -> x10, local copies, waits for them, and re-layouts: 70.3 us -> 2.64 us  [the longest x1 1.15 us: scatter_mlp(): blocks = own.reshape(ctx_count, rows // ctx_count, 128)]
    pallas_call x0 -> x10, Pallas kernels: none -> 59.1 us  [kernel_call(): pl.pallas_call(kernel, out_shape=[jax.ShapeDtypeStruct(shape, dtype) for...]
    dot_general x27 -> x0, matrix products: 53.6 us -> none  [the longest x7 16.3 us: left_dot(): lax.dot_general(left_cols, right_rows, (((0,), (0,)), ((), ())), preferre...]
    psum x1 -> x0, blocking collectives: 39.3 us -> none  [body(): lax.psum(jnp.stack([grad_gain_one, grad_gain_two]), ('dp', 'ctx'))]
  transfers between devices with their start and end apart: 11 -> 50, of which waited for: 3 -> 24; matrix products, arithmetic and copies ran while one was open for 19% -> 5% of each run, Pallas kernels for 0% -> 12%
where the time goes in v2:
time: 341 us; the launch traced here: 340 us
  waiting for transfers between devices  144 us (42%)
  starting transfers between devices  93.8 us (28%)
  Pallas kernels  59.1 us (17%)
  local copies, waits for them, and re-layouts  17.5 us (5%)
  between operations  14.6 us (4%)
  other arithmetic  10.5 us (3%)
    pallas_call x10, Pallas kernels, kernel_call(): pl.pallas_call(kernel, out_shape=[jax.ShapeDtypeStruct(shape, dtype) for...  59.1 us
    ppermute x18, starting transfers between devices, spread(): lax.ppermute(rows, 'ctx', swap_pairs('ctx', step))  42.6 us
    ppermute x18, waiting for transfers between devices, spread(): lax.ppermute(rows, 'ctx', swap_pairs('ctx', step))  42.1 us
    ppermute x6, waiting for transfers between devices, returned(): lax.ppermute(term, 'ctx', swap_pairs('ctx', step + 1))  29 us
    all_gather x1, waiting for transfers between devices, body_columns(): attn_whole = lax.all_gather(attn_near, 'dp', axis=0, tiled=True)  24.3 us
    ppermute x2, waiting for transfers between devices, body_columns(): lax.ppermute(kv_terms[back - step], 'ctx', down_pairs[step])  23.6 us
    ppermute x12, starting transfers between devices, trade(): got.append(lax.ppermute(block, 'ctx', swap_pairs('ctx', step)))  22.6 us
    ppermute x12, waiting for transfers between devices, trade(): got.append(lax.ppermute(block, 'ctx', swap_pairs('ctx', step)))  20.5 us
  transfers between devices with their start and end apart: 50, of which 24 were waited for; matrix products, arithmetic and copies ran while one was open for 5% of the time, Pallas kernels for 12%

profile of v2, /device:TPU:0, one launch (start us, length us, event | category | flops | bytes accessed | tf_op | source)
XLA Modules:
  0.0 340.0 jit_solution(13239656886750072511)
XLA Ops:
  7.2 5.1 %collective-permute-start.3 = (bf16[600,128]{1,0:T(8,128)(2,1)}, bf16[600,128]{1,0:T(8,128)(2,1)S(1)}, u32[]{:S(2)}, u32[]{:S(2)}) collective-permute-start(bf16[600,128]{1,0:T(8,128)(2,1)} %param.9), channel_id=1, source_target_pairs={{0,3},{1,2},{2,1},{3,0},{4,7},{5,6},{6,5},{7,4},{8,11},{9,10},{10,... | collective-permute-start | bytes 460808 | tf_op jit(solution)/shard_map/ppermute | solution.py:292
  13.0 4.5 %collective-permute-done.3 = bf16[600,128]{1,0:T(8,128)(2,1)S(1)} collective-permute-done((bf16[600,128]{1,0:T(8,128)(2,1)}, bf16[600,128]{1,0:T(8,128)(2,1)S(1)}, u32[]{:S(2)}, u32[]{:S(2)}) %collective-permute-start.3) | collective-permute-done | bytes 153632 | tf_op jit(solution)/shard_map/ppermute | solution.py:292
  17.5 8.1 %collective-permute-done.4 = bf16[600,128]{1,0:T(8,128)(2,1)S(1)} collective-permute-done((bf16[600,128]{1,0:T(8,128)(2,1)}, bf16[600,128]{1,0:T(8,128)(2,1)S(1)}, u32[]{:S(2)}, u32[]{:S(2)}) %collective-permute-start.4) | collective-permute-done | bytes 153632 | tf_op jit(solution)/shard_map/ppermute | solution.py:292
  34.8 3.4 collective-permute-done
  38.1 3.6 %collective-permute-done.1 = bf16[450,128]{1,0:T(8,128)(2,1)S(1)} collective-permute-done((bf16[450,128]{1,0:T(8,128)(2,1)S(1)}, bf16[450,128]{1,0:T(8,128)(2,1)S(1)}, u32[]{:S(2)}, u32[]{:S(2)}) %collective-permute-start.1) | collective-permute-done | bytes 115232 | tf_op jit(solution)/shard_map/ppermute | solution.py:307
  43.3 24.3 %all-gather.3.cloned.1.call-done.flat_ref = bf16[19200,128]{1,0:T(8,128)(2,1)} async-done(((bf16[2400,128]{1,0:T(8,128)(2,1)}), bf16[19200,128]{1,0:T(8,128)(2,1)}) %all-gather.3.cloned.1.call-update) | async-done | bytes 4915216 | tf_op jit(solution)/shard_map/all_gather | solution.py:1046
  75.5 8.7 %shard_map.118 = (bf16[128,960]{1,0:T(8,128)(2,1)}, bf16[128,960]{1,0:T(8,128)(2,1)}, bf16[128,640]{1,0:T(8,128)(2,1)}, bf16[960,1600]{1,0:T(8,128)(2,1)}, bf16[960,960]{1,0:T(8,128)(2,1)}) custom-call(bf16[19200,128]{1,0:T(8,128)(2,1)} %all-gather.3.cloned.1.call-done.flat_ref, f32[128,960]{1,0:T(8,128)} %bitcast.95, f32[1,960]{1,0:T(1,128)} %bitcast.125, ...), custom_call_target="tpu_custom_call" | custom-call | tf_op jit(solution)/shard_map/pallas_call | solution.py:396
  87.4 4.7 %collective-permute-start.7 = (bf16[128,640]{1,0:T(8,128)(2,1)}, bf16[128,640]{1,0:T(8,128)(2,1)S(1)}, u32[]{:S(2)}, u32[]{:S(2)}) collective-permute-start(bf16[128,640]{1,0:T(8,128)(2,1)} %get-tuple-element.46.refs_3_), channel_id=1, source_target_pairs={{0,1},{1,2},{2,3},{4,5},{5,6},{6,7},{8,9},{9,10},{10,11},{12,13},{... | collective-permute-start | bytes 491528 | tf_op jit(solution)/shard_map/ppermute | solution.py:1080
  95.7 6.0 %shard_map.119 = (bf16[384,640]{1,0:T(8,128)(2,1)}, bf16[128,960]{1,0:T(8,128)(2,1)}, f32[128,128]{1,0:T(8,128)}, f32[128,960]{1,0:T(8,128)}, bf16[128,960]{1,0:T(8,128)(2,1)}) custom-call(bf16[128,960]{1,0:T(8,128)(2,1)} %get-tuple-element.45.refs_0_.query_ref, bf16[128,640]{1,0:T(8,128)(2,1)} %copy-done.32, bf16[128,640]{1,0:T(8,128)(2,1)} %copy-done.33, ...), custom_call_target="tpu_custom_call" | custom-call | tf_op jit(solution)/shard_map/pallas_call | solution.py:396
  101.7 10.9 %collective-permute-start.10 = (bf16[128,960]{1,0:T(8,128)(2,1)}, bf16[128,960]{1,0:T(8,128)(2,1)S(1)}, u32[]{:S(2)}, u32[]{:S(2)}) collective-permute-start(bf16[128,960]{1,0:T(8,128)(2,1)} %get-tuple-element.49.refs_0_.refs_3_), channel_id=1, source_target_pairs={{0,3},{1,2},{2,1},{3,0},{4,7},{5,6},{6,5},{7,4},{8,11},{9,10},{10,... | collective-permute-start | bytes 737288 | tf_op jit(solution)/shard_map/ppermute | solution.py:292
  115.6 6.6 %shard_map.120 = (bf16[960,640]{1,0:T(8,128)(2,1)}, bf16[960,640]{1,0:T(8,128)(2,1)}, bf16[640,960]{1,0:T(8,128)(2,1)}, f32[512,640]{1,0:T(8,128)}) custom-call(bf16[14400,128]{1,0:T(8,128)(2,1)} %all-gather.5.cloned.1.call-done.flat_ref, bf16[128,960]{1,0:T(8,128)(2,1)} %copy-done.2, bf16[128,960]{1,0:T(8,128)(2,1)} %copy-done.5, ...), custom_call_target="tpu_custom_call" | custom-call | tf_op jit(solution)/shard_map/pallas_call | solution.py:396
  125.2 9.1 %collective-permute-done.9.refs_2_.refs_5_ = bf16[128,960]{1,0:T(8,128)(2,1)S(1)} collective-permute-done((bf16[128,960]{1,0:T(8,128)(2,1)}, bf16[128,960]{1,0:T(8,128)(2,1)S(1)}, u32[]{:S(2)}, u32[]{:S(2)}) %collective-permute-start.9) | collective-permute-done | bytes 245792 | tf_op jit(solution)/shard_map/ppermute | solution.py:292
  135.0 8.2 %shard_map.121 = (bf16[512,640]{1,0:T(8,128)(2,1)}, bf16[512,640]{1,0:T(8,128)(2,1)}, bf16[512,640]{1,0:T(8,128)(2,1)}, f32[128,960]{1,0:T(8,128)}, bf16[128,960...) custom-call(bf16[128,960]{1,0:T(8,128)(2,1)} %get-tuple-element.49.refs_0_.refs_3_, ...), custom_call_target="tpu_custom_call" | custom-call | tf_op jit(solution)/shard_map/pallas_call | solution.py:396
  143.2 8.8 %shard_map.122 = (bf16[14400,128]{1,0:T(8,128)(2,1)}, f32[128,960]{1,0:T(8,128)}, bf16[128,960]{1,0:T(8,128)(2,1)}, bf16[128,960]{1,0:T(8,128)(2,1)}, bf16[128,960]{1,0:T(8,128)(2,1)}) custom-call(bf16[512,640]{1,0:T(8,128)(2,1)} %get-tuple-element.54.refs_0_, bf16[512,640]{1,0:T(8,128)(2,1)} %get-tuple-element.55.refs_1_, ...), custom_call_target="tpu_custom_call" | custom-call | tf_op jit(solution)/shard_map/pallas_call | solution.py:396
  157.7 8.3 %collective-permute-done.17.refs_0_ = bf16[128,960]{1,0:T(8,128)(2,1)S(1)} collective-permute-done((bf16[128,960]{1,0:T(8,128)(2,1)S(1)}, bf16[128,960]{1,0:T(8,128)(2,1)S(1)}, u32[]{:S(2)}, u32[]{:S(2)}) %collective-permute-start.17) | collective-permute-done | bytes 245792 | tf_op jit(solution)/shard_map/ppermute | solution.py:298
  166.0 9.4 %collective-permute-done.18.refs_1_ = bf16[128,960]{1,0:T(8,128)(2,1)S(1)} collective-permute-done((bf16[128,960]{1,0:T(8,128)(2,1)S(1)}, bf16[128,960]{1,0:T(8,128)(2,1)S(1)}, u32[]{:S(2)}, u32[]{:S(2)}) %collective-permute-start.18) | collective-permute-done | bytes 245792 | tf_op jit(solution)/shard_map/ppermute | solution.py:298
  176.2 4.1 %shard_map.123 = (f32[128,960]{1,0:T(8,128)}, bf16[128,960]{1,0:T(8,128)(2,1)}, bf16[128,960]{1,0:T(8,128)(2,1)}, f32[1,960]{1,0:T(1,128)}) custom-call(f32[128,960]{1,0:T(8,128)} %get-tuple-element.63.own_ref, bf16[128,960]{1,0:T(8,128)(2,1)} %copy-done.22, bf16[128,960]{1,0:T(8,128)(2,1)} %copy-done.23, bf16[128,960]{1,0:T(8,128)(2,1)} %copy-done.24, ...), custom_call_target="tpu_custom_call" | custom-call | tf_op jit(solution)/shard_map/pallas_call | solution.py:396
  180.3 6.0 %shard_map.124 = (bf16[128,960]{1,0:T(8,128)(2,1)}, f32[128,640]{1,0:T(8,128)}, bf16[128,640]{1,0:T(8,128)(2,1)}, bf16[128,640]{1,0:T(8,128)(2,1)}) custom-call(bf16[128,960]{1,0:T(8,128)(2,1)} %get-tuple-element.45.refs_0_.query_ref, bf16[384,640]{1,0:T(8,128)(2,1)} %get-tuple-element.62.kv_ref, bf16[128,960]{1,0:T(8,128)(2,1)} %get-tuple-element.67.mix_ref, ...), custom_call_target="tpu_custom_call" | custom-call | tf_op jit(solution)/shard_map/pallas_call | solution.py:396
  187.8 5.8 %collective-permute-start.22 = (bf16[128,240]{1,0:T(8,128)(2,1)S(1)}, bf16[128,240]{1,0:T(8,128)(2,1)S(1)}, u32[]{:S(2)}, u32[]{:S(2)}) collective-permute-start(bf16[128,240]{1,0:T(8,128)(2,1)S(1)} %bitcast.121), channel_id=1, source_target_pairs={{0,1},{1,0},{2,3},{3,2},{4,5},{5,4},{6,7},{7,6},{8,9},{9,8},{10,11... | collective-permute-start | bytes 184328 | tf_op jit(solution)/shard_map/ppermute | solution.py:307
  209.4 3.4 %collective-permute-start.29 = (bf16[128,960]{1,0:T(8,128)(2,1)}, bf16[128,960]{1,0:T(8,128)(2,1)S(1)}, u32[]{:S(2)}, u32[]{:S(2)}) collective-permute-start(bf16[128,960]{1,0:T(8,128)(2,1)} %get-tuple-element.69.query_ref.refs_8_), channel_id=1, source_target_pairs={{0,2},{1,3},{2,0},{3,1},{4,6},{5,7},{6,4},{7,5},{8,10},{9,11},{10,... | collective-permute-start | bytes 737288 | tf_op jit(solution)/shard_map/ppermute | solution.py:292
  215.2 3.8 %collective-permute-start.30 = (bf16[128,960]{1,0:T(8,128)(2,1)}, bf16[128,960]{1,0:T(8,128)(2,1)S(1)}, u32[]{:S(2)}, u32[]{:S(2)}) collective-permute-start(bf16[128,960]{1,0:T(8,128)(2,1)} %get-tuple-element.69.query_ref.refs_8_), channel_id=1, source_target_pairs={{0,3},{1,2},{2,1},{3,0},{4,7},{5,6},{6,5},{7,4},{8,11},{9,10},{10,... | collective-permute-start | bytes 737288 | tf_op jit(solution)/shard_map/ppermute | solution.py:292
  219.0 23.6 %collective-permute-done.21.refs_1_ = bf16[128,640]{1,0:T(8,128)(2,1)S(1)} collective-permute-done((bf16[128,640]{1,0:T(8,128)(2,1)}, bf16[128,640]{1,0:T(8,128)(2,1)S(1)}, u32[]{:S(2)}, u32[]{:S(2)}) %collective-permute-start.21) | collective-permute-done | bytes 163872 | tf_op jit(solution)/shard_map/ppermute | solution.py:1109
  248.1 5.0 %collective-permute-start.32 = (bf16[128,640]{1,0:T(8,128)(2,1)}, bf16[128,640]{1,0:T(8,128)(2,1)S(1)}, u32[]{:S(2)}, u32[]{:S(2)}) collective-permute-start(bf16[128,640]{1,0:T(8,128)(2,1)} %shard_map.125.kv_ref.refs_12_), channel_id=1, source_target_pairs={{0,2},{1,3},{2,0},{3,1},{4,6},{5,7},{6,4},{7,5},{8,10},{9,11},{10,... | collective-permute-start | bytes 491528 | tf_op jit(solution)/shard_map/ppermute | solution.py:292
  253.1 3.7 %collective-permute-start.33 = (bf16[128,640]{1,0:T(8,128)(2,1)}, bf16[128,640]{1,0:T(8,128)(2,1)S(1)}, u32[]{:S(2)}, u32[]{:S(2)}) collective-permute-start(bf16[128,640]{1,0:T(8,128)(2,1)} %shard_map.125.kv_ref.refs_12_), channel_id=1, source_target_pairs={{0,3},{1,2},{2,1},{3,0},{4,7},{5,6},{6,5},{7,4},{8,11},{9,10},{10,... | collective-permute-start | bytes 491528 | tf_op jit(solution)/shard_map/ppermute | solution.py:292
  258.3 8.2 %collective-permute-done.35.refs_18_ = bf16[128,960]{1,0:T(8,128)(2,1)S(1)} collective-permute-done((bf16[128,960]{1,0:T(8,128)(2,1)S(1)}, bf16[128,960]{1,0:T(8,128)(2,1)S(1)}, u32[]{:S(2)}, u32[]{:S(2)}) %collective-permute-start.35) | collective-permute-done | bytes 245792 | tf_op jit(solution)/shard_map/ppermute | solution.py:292
  266.5 9.1 %collective-permute-done.32.refs_14_ = bf16[128,640]{1,0:T(8,128)(2,1)S(1)} collective-permute-done((bf16[128,640]{1,0:T(8,128)(2,1)}, bf16[128,640]{1,0:T(8,128)(2,1)S(1)}, u32[]{:S(2)}, u32[]{:S(2)}) %collective-permute-start.32) | collective-permute-done | bytes 163872 | tf_op jit(solution)/shard_map/ppermute | solution.py:292
  276.4 4.2 %shard_map.127 = bf16[4800,128]{1,0:T(8,128)(2,1)} custom-call(bf16[128,240]{1,0:T(8,128)(2,1)} %bitcast.111, bf16[128,240]{1,0:T(8,128)(2,1)} %copy-done.34, bf16[128,240]{1,0:T(8,128)(2,1)} %copy-done.35, bf16[128,240]{1,0:T(8,128)(2,1)} %copy-done.36, bf16[128,240]{1,0:T(8,128)(2,1)} %bitcast.112, bf16[128,240]{1,0:T(8,128)(2,1)} %copy-done.37, ...), custom_call_target="tpu_custom_call" | custom-call | tf_op jit(solution)/shard_map/pallas_call | solution.py:396
  280.6 4.5 %shard_map.126 = (f32[128,960]{1,0:T(8,128)}, f32[1,960]{1,0:T(1,128)}) custom-call(bf16[128,960]{1,0:T(8,128)(2,1)} %get-tuple-element.69.query_ref.refs_8_, bf16[128,640]{1,0:T(8,128)(2,1)} %shard_map.125.kv_ref.refs_12_, bf16[960,1600]{1,0:T(8,128)(2,1)} %get-tuple-element.73.w_ref, f32[128,960]{1,0:T(8,128)} %bitcast.97, f32[1,960]{1,0:T(1,128)} %bitcast.126, ...), custom_call_target="tpu_custom_call" | custom-call | tf_op jit(solution)/shard_map/pallas_call | solution.py:396
  285.9 3.8 %collective-permute-start.40 = (f32[2,960]{1,0:T(2,128)S(1)}, f32[2,960]{1,0:T(2,128)S(1)}, u32[]{:S(2)}, u32[]{:S(2)}) collective-permute-start(f32[2,960]{1,0:T(2,128)S(1)} %pad_maximum_fusion.8), channel_id=1, source_target_pairs={{0,1},{1,0},{2,3},{3,2},{4,5},{5,4},{6,7},{7,6},{8,9},{9,8},{10,11... | collective-permute-start | bytes 23048 | tf_op jit(solution)/shard_map/ppermute | solution.py:278
  303.6 11.0 %collective-permute-done.15 = bf16[128,960]{1,0:T(8,128)(2,1)S(1)} collective-permute-done((bf16[128,960]{1,0:T(8,128)(2,1)S(1)}, bf16[128,960]{1,0:T(8,128)(2,1)S(1)}, u32[]{:S(2)}, u32[]{:S(2)}) %collective-permute-start.15) | collective-permute-done | bytes 245792 | tf_op jit(solution)/shard_map/ppermute | solution.py:298
  318.9 5.7 %collective-permute-start.38 = (bf16[450,128]{1,0:T(8,128)(2,1)S(1)}, bf16[450,128]{1,0:T(8,128)(2,1)S(1)}, u32[]{:S(2)}, u32[]{:S(2)}) collective-permute-start(bf16[450,128]{1,0:T(8,128)(2,1)S(1)} %get-tuple-element.131), channel_id=1, source_target_pairs={{0,2},{1,3},{2,0},{3,1},{4,6},{5,7},{6,4},{7,5},{8,10},{9,11},{10,... | collective-permute-start | bytes 345608 | tf_op jit(solution)/shard_map/ppermute | solution.py:307
  327.1 3.6 %collective-permute-done.38 = bf16[450,128]{1,0:T(8,128)(2,1)S(1)} collective-permute-done((bf16[450,128]{1,0:T(8,128)(2,1)S(1)}, bf16[450,128]{1,0:T(8,128)(2,1)S(1)}, u32[]{:S(2)}, u32[]{:S(2)}) %collective-permute-start.38) | collective-permute-done | bytes 115232 | tf_op jit(solution)/shard_map/ppermute | solution.py:307
  (252 shorter events, 90.4 us)
Async XLA Ops:
  7.2 60.4 %all-gather.3.cloned.1.call-start = ((), (), s32[]{:S(2)}) async-start(), calls=%async_computation.2 | async-start | bytes 5529600 | tf_op jit(solution)/shard_map/all_gather | solution.py:1046
  12.3 13.2 %collective-permute-start.4 = (bf16[600,128]{1,0:T(8,128)(2,1)}, bf16[600,128]{1,0:T(8,128)(2,1)S(1)}, u32[]{:S(2)}, u32[]{:S(2)}) collective-permute-start(bf16[600,128]{1,0:T(8,128)(2,1)} %param.9), channel_id=1, source_target_pairs={{0,2},{1,3},{2,0},{3,1},{4,6},{5,7},{6,4},{7,5},{8,10},{9,11},{10,... | collective-permute-start | bytes 460808 | tf_op jit(solution)/shard_map/ppermute | solution.py:292
  12.3 13.2 %collective-permute-start.5 = (bf16[600,128]{1,0:T(8,128)(2,1)}, bf16[600,128]{1,0:T(8,128)(2,1)S(1)}, u32[]{:S(2)}, u32[]{:S(2)}) collective-permute-start(bf16[600,128]{1,0:T(8,128)(2,1)} %param.9), channel_id=1, source_target_pairs={{0,1},{1,0},{2,3},{3,2},{4,5},{5,4},{6,7},{7,6},{8,9},{9,8},{10,11... | collective-permute-start | bytes 460808 | tf_op jit(solution)/shard_map/ppermute | solution.py:292
  27.6 87.2 %all-gather.5.cloned.1.call-start = ((), (), s32[]{:S(2)}) async-start(), calls=%async_computation.3 | async-start | bytes 4147200 | tf_op jit(solution)/shard_map/all_gather | solution.py:1048
  67.6 249.1 %reduce-scatter.9.cloned.1.call-start = ((), (), s32[]{:S(2)}) async-start(), calls=%async_computation.5 | async-start | bytes 4147200
  67.9 46.7 %collective-permute-start.11 = (bf16[128,960]{1,0:T(8,128)(2,1)S(1)}, bf16[128,960]{1,0:T(8,128)(2,1)S(1)}, u32[]{:S(2)}, u32[]{:S(2)}) collective-permute-start(bf16[128,960]{1,0:T(8,128)(2,1)S(1)} %bitcast_convert_fusion.refs_0_.refs_7_), channel_id=1, source_target_pairs={{0,1},{1,0},{2,3},{3,2},{4,5},{5,4},{6,7},{7,6},{8,9},{9,8},{10,11... | collective-permute-start | bytes 737288 | tf_op jit(solution)/shard_map/ppermute | solution.py:292
  69.5 45.2 %collective-permute-start.12 = (bf16[128,960]{1,0:T(8,128)(2,1)S(1)}, bf16[128,960]{1,0:T(8,128)(2,1)S(1)}, u32[]{:S(2)}, u32[]{:S(2)}) collective-permute-start(bf16[128,960]{1,0:T(8,128)(2,1)S(1)} %bitcast_convert_fusion.refs_0_.refs_7_), channel_id=1, source_target_pairs={{0,2},{1,3},{2,0},{3,1},{4,6},{5,7},{6,4},{7,5},{8,10},{9,11},{10,... | collective-permute-start | bytes 737288 | tf_op jit(solution)/shard_map/ppermute | solution.py:292
  71.9 42.8 %collective-permute-start.13 = (bf16[128,960]{1,0:T(8,128)(2,1)S(1)}, bf16[128,960]{1,0:T(8,128)(2,1)S(1)}, u32[]{:S(2)}, u32[]{:S(2)}) collective-permute-start(bf16[128,960]{1,0:T(8,128)(2,1)S(1)} %bitcast_convert_fusion.refs_0_.refs_7_), channel_id=1, source_target_pairs={{0,3},{1,2},{2,1},{3,0},{4,7},{5,6},{6,5},{7,4},{8,11},{9,10},{10,... | collective-permute-start | bytes 737288 | tf_op jit(solution)/shard_map/ppermute | solution.py:292
  101.7 20.4 %collective-permute-start.10 = (bf16[128,960]{1,0:T(8,128)(2,1)}, bf16[128,960]{1,0:T(8,128)(2,1)S(1)}, u32[]{:S(2)}, u32[]{:S(2)}) collective-permute-start(bf16[128,960]{1,0:T(8,128)(2,1)} %get-tuple-element.49.refs_0_.refs_3_), channel_id=1, source_target_pairs={{0,3},{1,2},{2,1},{3,0},{4,7},{5,6},{6,5},{7,4},{8,11},{9,10},{10,... | collective-permute-start | bytes 737288 | tf_op jit(solution)/shard_map/ppermute | solution.py:292
  112.6 12.6 %collective-permute-start.8 = (bf16[128,960]{1,0:T(8,128)(2,1)}, bf16[128,960]{1,0:T(8,128)(2,1)S(1)}, u32[]{:S(2)}, u32[]{:S(2)}) collective-permute-start(bf16[128,960]{1,0:T(8,128)(2,1)} %get-tuple-element.49.refs_0_.refs_3_), channel_id=1, source_target_pairs={{0,1},{1,0},{2,3},{3,2},{4,5},{5,4},{6,7},{7,6},{8,9},{9,8},{10,11... | collective-permute-start | bytes 737288 | tf_op jit(solution)/shard_map/ppermute | solution.py:292
  114.7 19.6 %collective-permute-start.9 = (bf16[128,960]{1,0:T(8,128)(2,1)}, bf16[128,960]{1,0:T(8,128)(2,1)S(1)}, u32[]{:S(2)}, u32[]{:S(2)}) collective-permute-start(bf16[128,960]{1,0:T(8,128)(2,1)} %get-tuple-element.49.refs_0_.refs_3_), channel_id=1, source_target_pairs={{0,2},{1,3},{2,0},{3,1},{4,6},{5,7},{6,4},{7,5},{8,10},{9,11},{10,... | collective-permute-start | bytes 737288 | tf_op jit(solution)/shard_map/ppermute | solution.py:292
  152.0 173.2 %reduce-scatter.7.cloned.1.call-start = ((), (), s32[]{:S(2)}) async-start(), calls=%async_computation.4 | async-start | bytes 1382400
  152.9 13.1 %collective-permute-start.17 = (bf16[128,960]{1,0:T(8,128)(2,1)S(1)}, bf16[128,960]{1,0:T(8,128)(2,1)S(1)}, u32[]{:S(2)}, u32[]{:S(2)}) collective-permute-start(bf16[128,960]{1,0:T(8,128)(2,1)S(1)} %copy-done.47), channel_id=1, source_target_pairs={{0,1},{1,0},{2,3},{3,2},{4,5},{5,4},{6,7},{7,6},{8,9},{9,8},{10,11... | collective-permute-start | bytes 737288 | tf_op jit(solution)/shard_map/ppermute | solution.py:298
  153.8 21.7 %collective-permute-start.18 = (bf16[128,960]{1,0:T(8,128)(2,1)S(1)}, bf16[128,960]{1,0:T(8,128)(2,1)S(1)}, u32[]{:S(2)}, u32[]{:S(2)}) collective-permute-start(bf16[128,960]{1,0:T(8,128)(2,1)S(1)} %copy-done.46), channel_id=1, source_target_pairs={{0,2},{1,3},{2,0},{3,1},{4,6},{5,7},{6,4},{7,5},{8,10},{9,11},{10,... | collective-permute-start | bytes 737288 | tf_op jit(solution)/shard_map/ppermute | solution.py:298
  157.0 18.4 %collective-permute-start.19 = (bf16[128,960]{1,0:T(8,128)(2,1)S(1)}, bf16[128,960]{1,0:T(8,128)(2,1)S(1)}, u32[]{:S(2)}, u32[]{:S(2)}) collective-permute-start(bf16[128,960]{1,0:T(8,128)(2,1)S(1)} %copy-done.45), channel_id=1, source_target_pairs={{0,3},{1,2},{2,1},{3,0},{4,7},{5,6},{6,5},{7,4},{8,11},{9,10},{10,... | collective-permute-start | bytes 737288 | tf_op jit(solution)/shard_map/ppermute | solution.py:298
  186.3 32.6 %collective-permute-start.20 = (bf16[128,640]{1,0:T(8,128)(2,1)}, bf16[128,640]{1,0:T(8,128)(2,1)S(1)}, u32[]{:S(2)}, u32[]{:S(2)}) collective-permute-start(bf16[128,640]{1,0:T(8,128)(2,1)} %get-tuple-element.71), channel_id=1, source_target_pairs={{1,0},{2,1},{3,2},{5,4},{6,5},{7,6},{9,8},{10,9},{11,10},{13,12},{... | collective-permute-start | bytes 491528 | tf_op jit(solution)/shard_map/ppermute | solution.py:1109
  187.8 12.2 %collective-permute-start.22 = (bf16[128,240]{1,0:T(8,128)(2,1)S(1)}, bf16[128,240]{1,0:T(8,128)(2,1)S(1)}, u32[]{:S(2)}, u32[]{:S(2)}) collective-permute-start(bf16[128,240]{1,0:T(8,128)(2,1)S(1)} %bitcast.121), channel_id=1, source_target_pairs={{0,1},{1,0},{2,3},{3,2},{4,5},{5,4},{6,7},{7,6},{8,9},{9,8},{10,11... | collective-permute-start | bytes 184328 | tf_op jit(solution)/shard_map/ppermute | solution.py:307
  196.9 45.7 %collective-permute-start.28 = (bf16[128,960]{1,0:T(8,128)(2,1)}, bf16[128,960]{1,0:T(8,128)(2,1)S(1)}, u32[]{:S(2)}, u32[]{:S(2)}) collective-permute-start(bf16[128,960]{1,0:T(8,128)(2,1)} %get-tuple-element.69.query_ref.refs_8_), channel_id=1, source_target_pairs={{0,1},{1,0},{2,3},{3,2},{4,5},{5,4},{6,7},{7,6},{8,9},{9,8},{10,11... | collective-permute-start | bytes 737288 | tf_op jit(solution)/shard_map/ppermute | solution.py:292
  209.4 35.9 %collective-permute-start.29 = (bf16[128,960]{1,0:T(8,128)(2,1)}, bf16[128,960]{1,0:T(8,128)(2,1)S(1)}, u32[]{:S(2)}, u32[]{:S(2)}) collective-permute-start(bf16[128,960]{1,0:T(8,128)(2,1)} %get-tuple-element.69.query_ref.refs_8_), channel_id=1, source_target_pairs={{0,2},{1,3},{2,0},{3,1},{4,6},{5,7},{6,4},{7,5},{8,10},{9,11},{10,... | collective-permute-start | bytes 737288 | tf_op jit(solution)/shard_map/ppermute | solution.py:292
  212.8 29.8 %collective-permute-start.21 = (bf16[128,640]{1,0:T(8,128)(2,1)}, bf16[128,640]{1,0:T(8,128)(2,1)S(1)}, u32[]{:S(2)}, u32[]{:S(2)}) collective-permute-start(bf16[128,640]{1,0:T(8,128)(2,1)} %get-tuple-element.72), channel_id=1, source_target_pairs={{2,0},{3,1},{6,4},{7,5},{10,8},{11,9},{14,12},{15,13},{18,16},{19,... | collective-permute-start | bytes 491528 | tf_op jit(solution)/shard_map/ppermute | solution.py:1109
  215.2 32.9 %collective-permute-start.30 = (bf16[128,960]{1,0:T(8,128)(2,1)}, bf16[128,960]{1,0:T(8,128)(2,1)S(1)}, u32[]{:S(2)}, u32[]{:S(2)}) collective-permute-start(bf16[128,960]{1,0:T(8,128)(2,1)} %get-tuple-element.69.query_ref.refs_8_), channel_id=1, source_target_pairs={{0,3},{1,2},{2,1},{3,0},{4,7},{5,6},{6,5},{7,4},{8,11},{9,10},{10,... | collective-permute-start | bytes 737288 | tf_op jit(solution)/shard_map/ppermute | solution.py:292
  219.0 34.1 %collective-permute-start.34 = (bf16[128,960]{1,0:T(8,128)(2,1)S(1)}, bf16[128,960]{1,0:T(8,128)(2,1)S(1)}, u32[]{:S(2)}, u32[]{:S(2)}) collective-permute-start(bf16[128,960]{1,0:T(8,128)(2,1)S(1)} %copy-done.15), channel_id=1, source_target_pairs={{0,1},{1,0},{2,3},{3,2},{4,5},{5,4},{6,7},{7,6},{8,9},{9,8},{10,11... | collective-permute-start | bytes 737288 | tf_op jit(solution)/shard_map/ppermute | solution.py:292
  242.6 23.9 %collective-permute-start.35 = (bf16[128,960]{1,0:T(8,128)(2,1)S(1)}, bf16[128,960]{1,0:T(8,128)(2,1)S(1)}, u32[]{:S(2)}, u32[]{:S(2)}) collective-permute-start(bf16[128,960]{1,0:T(8,128)(2,1)S(1)} %copy-done.15), channel_id=1, source_target_pairs={{0,2},{1,3},{2,0},{3,1},{4,6},{5,7},{6,4},{7,5},{8,10},{9,11},{10,... | collective-permute-start | bytes 737288 | tf_op jit(solution)/shard_map/ppermute | solution.py:292
  242.6 23.9 %collective-permute-start.36 = (bf16[128,960]{1,0:T(8,128)(2,1)S(1)}, bf16[128,960]{1,0:T(8,128)(2,1)S(1)}, u32[]{:S(2)}, u32[]{:S(2)}) collective-permute-start(bf16[128,960]{1,0:T(8,128)(2,1)S(1)} %copy-done.15), channel_id=1, source_target_pairs={{0,3},{1,2},{2,1},{3,0},{4,7},{5,6},{6,5},{7,4},{8,11},{9,10},{10,... | collective-permute-start | bytes 737288 | tf_op jit(solution)/shard_map/ppermute | solution.py:292
  245.3 21.2 %collective-permute-start.31 = (bf16[128,640]{1,0:T(8,128)(2,1)}, bf16[128,640]{1,0:T(8,128)(2,1)S(1)}, u32[]{:S(2)}, u32[]{:S(2)}) collective-permute-start(bf16[128,640]{1,0:T(8,128)(2,1)} %shard_map.125.kv_ref.refs_12_), channel_id=1, source_target_pairs={{0,1},{1,0},{2,3},{3,2},{4,5},{5,4},{6,7},{7,6},{8,9},{9,8},{10,11... | collective-permute-start | bytes 491528 | tf_op jit(solution)/shard_map/ppermute | solution.py:292
  248.1 27.5 %collective-permute-start.32 = (bf16[128,640]{1,0:T(8,128)(2,1)}, bf16[128,640]{1,0:T(8,128)(2,1)S(1)}, u32[]{:S(2)}, u32[]{:S(2)}) collective-permute-start(bf16[128,640]{1,0:T(8,128)(2,1)} %shard_map.125.kv_ref.refs_12_), channel_id=1, source_target_pairs={{0,2},{1,3},{2,0},{3,1},{4,6},{5,7},{6,4},{7,5},{8,10},{9,11},{10,... | collective-permute-start | bytes 491528 | tf_op jit(solution)/shard_map/ppermute | solution.py:292
  253.1 22.5 %collective-permute-start.33 = (bf16[128,640]{1,0:T(8,128)(2,1)}, bf16[128,640]{1,0:T(8,128)(2,1)S(1)}, u32[]{:S(2)}, u32[]{:S(2)}) collective-permute-start(bf16[128,640]{1,0:T(8,128)(2,1)} %shard_map.125.kv_ref.refs_12_), channel_id=1, source_target_pairs={{0,3},{1,2},{2,1},{3,0},{4,7},{5,6},{6,5},{7,4},{8,11},{9,10},{10,... | collective-permute-start | bytes 491528 | tf_op jit(solution)/shard_map/ppermute | solution.py:292
  292.2 11.5 %collective-permute-start.14 = (bf16[128,960]{1,0:T(8,128)(2,1)S(1)}, bf16[128,960]{1,0:T(8,128)(2,1)S(1)}, u32[]{:S(2)}, u32[]{:S(2)}) collective-permute-start(bf16[128,960]{1,0:T(8,128)(2,1)S(1)} %copy-done.44), channel_id=1, source_target_pairs={{0,1},{1,0},{2,3},{3,2},{4,5},{5,4},{6,7},{7,6},{8,9},{9,8},{10,11... | collective-permute-start | bytes 737288 | tf_op jit(solution)/shard_map/ppermute | solution.py:298
  293.2 21.4 %collective-permute-start.15 = (bf16[128,960]{1,0:T(8,128)(2,1)S(1)}, bf16[128,960]{1,0:T(8,128)(2,1)S(1)}, u32[]{:S(2)}, u32[]{:S(2)}) collective-permute-start(bf16[128,960]{1,0:T(8,128)(2,1)S(1)} %copy-done.43), channel_id=1, source_target_pairs={{0,2},{1,3},{2,0},{3,1},{4,6},{5,7},{6,4},{7,5},{8,10},{9,11},{10,... | collective-permute-start | bytes 737288 | tf_op jit(solution)/shard_map/ppermute | solution.py:298
  294.1 20.5 %collective-permute-start.16 = (bf16[128,960]{1,0:T(8,128)(2,1)S(1)}, bf16[128,960]{1,0:T(8,128)(2,1)S(1)}, u32[]{:S(2)}, u32[]{:S(2)}) collective-permute-start(bf16[128,960]{1,0:T(8,128)(2,1)S(1)} %copy-done.42), channel_id=1, source_target_pairs={{0,3},{1,2},{2,1},{3,0},{4,7},{5,6},{6,5},{7,4},{8,11},{9,10},{10,... | collective-permute-start | bytes 737288 | tf_op jit(solution)/shard_map/ppermute | solution.py:298
  302.2 14.6 %collective-permute-start.45 = (f32[2,960]{1,0:T(2,128)S(1)}, f32[2,960]{1,0:T(2,128)S(1)}, u32[]{:S(2)}, u32[]{:S(2)}) collective-permute-start(f32[2,960]{1,0:T(2,128)S(1)} %add.83), channel_id=1, source_target_pairs={{0,16},{4,20},{8,24},{12,28},{16,0},{20,4},{24,8},{28,12},{1,17},{... | collective-permute-start | bytes 23048 | tf_op jit(solution)/shard_map/ppermute | solution.py:281
  318.9 11.7 %collective-permute-start.38 = (bf16[450,128]{1,0:T(8,128)(2,1)S(1)}, bf16[450,128]{1,0:T(8,128)(2,1)S(1)}, u32[]{:S(2)}, u32[]{:S(2)}) collective-permute-start(bf16[450,128]{1,0:T(8,128)(2,1)S(1)} %get-tuple-element.131), channel_id=1, source_target_pairs={{0,2},{1,3},{2,0},{3,1},{4,6},{5,7},{6,4},{7,5},{8,10},{9,11},{10,... | collective-permute-start | bytes 345608 | tf_op jit(solution)/shard_map/ppermute | solution.py:307
  (68 other events, 1097.8 us)
Sparse Core Ops, SparseCore 0:
  27.7 39.8 all-gather.2
  70.1 34.5 all-gather.4
  152.2 49.2 reduce-scatter.8
  280.7 37.0 reduce-scatter.6
